TPU v7x, 32 devices: a whole 2x2x4 slice. The times are simulated.
32 devices in a mesh: fsdp: 8 (over y, x, core), tp: 4 (over z).
Axes of the slice: x: 2, y: 2, z: 4, core: 2. Of those that a mesh axis runs over, the one named last changes fastest.
Arguments:
- layer_input: bfloat16 [8192, 2048], P(('fsdp', 'tp')), may hold values from -6 to 6
- segments: int32 [16, 512], P('fsdp'), may hold values from 0 to 7, never falling along the last dimension, each value on 1 to 256 neighbouring positions
- cotangent: bfloat16 [8192, 2048], P(('fsdp', 'tp')), may hold values from -6 to 6
- attention_gain: float32 [2048], replicated, may hold values from 0.1 to 1.9
- query_weight: bfloat16 [2048, 2048], P('fsdp', 'tp'), may hold values from -0.125 to 0.125
- key_matrix: bfloat16 [2048, 1024], P('fsdp', 'tp'), may hold values from -0.125 to 0.125
- value_matrix: bfloat16 [2048, 1024], P('fsdp', 'tp'), may hold values from -0.125 to 0.125
- query_norm_gain: float32 [128], replicated, may hold values from 0.1 to 1.9
- key_gain: float32 [128], replicated, may hold values from 0.1 to 1.9
- output_matrix: bfloat16 [2048, 2048], P('tp', 'fsdp'), may hold values from -1 to 1
- hidden_gain: float32 [2048], replicated, may hold values from 0.1 to 1.9
- gate_weight: bfloat16 [2048, 6144], P('fsdp', 'tp'), may hold values from -0.125 to 0.125
- up_weight: bfloat16 [2048, 6144], P('fsdp', 'tp'), may hold values from -0.125 to 0.125
- down_weight: bfloat16 [6144, 2048], P('tp', 'fsdp'), may hold values from -0.078125 to 0.078125
Outputs:
- layer_output: bfloat16 [8192, 2048], P(('fsdp', 'tp'))
- input_gradient: bfloat16 [8192, 2048], P(('fsdp', 'tp'))
- attention_gain_gradient: float32 [2048], replicated
- query_weight_gradient: float32 [2048, 2048], P('fsdp', 'tp')
- key_weight_gradient: float32 [2048, 1024], P('fsdp', 'tp')
- value_weight_gradient: float32 [2048, 1024], P('fsdp', 'tp')
- query_gain_gradient: float32 [128], replicated
- key_gain_gradient: float32 [128], replicated
- output_weight_gradient: float32 [2048, 2048], P('tp', 'fsdp')
- hidden_gain_gradient: float32 [2048], replicated
- gate_weight_gradient: float32 [2048, 6144], P('fsdp', 'tp')
- up_weight_gradient: float32 [2048, 6144], P('fsdp', 'tp')
- down_weight_gradient: float32 [6144, 2048], P('tp', 'fsdp')
Inputs may be any that keep to these rules, and one draw needn't show every extreme that they name: `segments`: within each sequence the ids never fall along positions and all 8 ids occur; each document holds 1 to 256 tokens, and some document holds exactly 256.
All inputs are finite; a program needn't handle non-finite values.
Results may differ from a plain program's by a relative error of at most 0.014.
Values may be sent and summed in bfloat16 or wider, within the bound.
No kernel may reach another device: no remote copies, remote signals or barrier semaphores. Data moves between devices by JAX's collectives and lax.ppermute only.
A program may use at most 256 MiB of HBM per device.

v0:
```python
from functools import partial
import math

import jax
import jax.numpy as jnp
from jax import lax
from jax.sharding import PartitionSpec as P

HEAD_SIZE = 128


EPSILON = 1e-06
THETA = 1000000.0


def rms_scale(value_rows, norm_gain):
    return (
        value_rows
        * lax.rsqrt(jnp.mean(value_rows * value_rows, axis=-1, keepdims=True) + EPSILON)
        * norm_gain
    )


def doc_positions(segments):
    length = segments.shape[-1]
    indices = jnp.arange(length, dtype=jnp.int32)
    leading = jnp.ones(segments.shape[:-1] + (1,), dtype=jnp.bool_)
    change = jnp.concatenate([leading, segments[..., 1:] != segments[..., :-1]], axis=-1)
    starts = lax.cummax(jnp.where(change, indices, jnp.int32(0)), axis=segments.ndim - 1)
    return indices - starts


def rotate(vectors, token_positions):
    half_dim = vectors.shape[-1] // 2
    exponents = jnp.arange(half_dim, dtype=jnp.float32) * (-2.0 / vectors.shape[-1])
    frequencies = jnp.power(jnp.float32(THETA), exponents)
    angles = token_positions.astype(jnp.float32)[..., None] * frequencies
    cosine_table = jnp.cos(angles)[..., None, :]
    sine_table = jnp.sin(angles)[..., None, :]
    first_half = vectors[..., :half_dim]
    second_half = vectors[..., half_dim:]
    return jnp.concatenate(
        [
            first_half * cosine_table - second_half * sine_table,
            second_half * cosine_table + first_half * sine_table,
        ],
        axis=-1,
    )


def head_lookup(raw_heads, norm_gain, token_positions):
    return rotate(rms_scale(raw_heads, norm_gain), token_positions)


def contract_product(left_side, right_side, left_dim, right_dim):
    return lax.dot_general(
        left_side,
        right_side,
        (((left_dim,), (right_dim,)), ((), ())),
        preferred_element_type=jnp.float32,
    )


def attend_mask(segments):
    length = segments.shape[0]
    indices = jnp.arange(length, dtype=jnp.int32)
    causal = indices[:, None] >= indices[None, :]
    return causal & (segments[:, None] == segments[None, :])


def attend_forward(query_rows, keys, value_rows, segments):
    score_scale = 1.0 / math.sqrt(query_rows.shape[-1])
    scores = (
        jnp.einsum("qkgd,ckd->kgqc", query_rows, keys, preferred_element_type=jnp.float32)
        * score_scale
    )
    allowed = attend_mask(segments)
    exponent = jnp.where(allowed, jnp.exp(scores), 0.0)
    log_total = jnp.log(jnp.sum(exponent, axis=-1))
    probability = jnp.where(allowed, jnp.exp(scores - log_total[..., None]), 0.0).astype(
        jnp.bfloat16
    )
    attended = jnp.einsum(
        "kgqc,ckd->qkgd", probability, value_rows, preferred_element_type=jnp.float32
    ).astype(jnp.bfloat16)
    return (attended, log_total)


def attend_backward(query_rows, keys, value_rows, segments, log_total, attended, attended_gradient):
    score_scale = 1.0 / math.sqrt(query_rows.shape[-1])
    scores = (
        jnp.einsum("qkgd,ckd->kgqc", query_rows, keys, preferred_element_type=jnp.float32)
        * score_scale
    )
    allowed = attend_mask(segments)
    probability = jnp.where(allowed, jnp.exp(scores - log_total[..., None]), 0.0)
    prob_low = probability.astype(jnp.bfloat16)
    delta = jnp.einsum(
        "qkgd,qkgd->kgq", attended_gradient, attended, preferred_element_type=jnp.float32
    )
    value_dots = jnp.einsum(
        "qkgd,ckd->kgqc", attended_gradient, value_rows, preferred_element_type=jnp.float32
    )
    score_back = (probability * (value_dots - delta[..., None])).astype(jnp.bfloat16)
    query_back = (
        jnp.einsum("kgqc,ckd->qkgd", score_back, keys, preferred_element_type=jnp.float32)
        * score_scale
    )
    key_back = (
        jnp.einsum("kgqc,qkgd->ckd", score_back, query_rows, preferred_element_type=jnp.float32)
        * score_scale
    )
    value_gradient = jnp.einsum(
        "kgqc,qkgd->ckd", prob_low, attended_gradient, preferred_element_type=jnp.float32
    ).astype(jnp.bfloat16)
    return (query_back, key_back, value_gradient)


def forward_item(items):
    return attend_forward(items[0], items[1], items[2], items[3])


def backward_item(items):
    return attend_backward(items[0], items[1], items[2], items[3], items[4], items[5], items[6])


def shards(
    layer_input,
    segments,
    cotangent,
    attention_gain,
    query_weight,
    key_matrix,
    value_matrix,
    query_norm_gain,
    key_gain,
    output_matrix,
    hidden_gain,
    gate_weight,
    up_weight,
    down_weight,
):
    input_float = layer_input.astype(jnp.float32)
    attention_input = rms_scale(input_float, attention_gain).astype(jnp.bfloat16)
    query_full, key_full, value_full, output_full = (
        lax.all_gather(query_weight, "fsdp", axis=0, tiled=True),
        lax.all_gather(key_matrix, "fsdp", axis=0, tiled=True),
        lax.all_gather(value_matrix, "fsdp", axis=0, tiled=True),
        lax.all_gather(output_matrix, "fsdp", axis=1, tiled=True),
    )
    gate_full, up_full, down_full = (
        lax.all_gather(gate_weight, "fsdp", axis=0, tiled=True),
        lax.all_gather(up_weight, "fsdp", axis=0, tiled=True),
        lax.all_gather(down_weight, "fsdp", axis=1, tiled=True),
    )
    attention_rows = lax.all_gather(attention_input, "tp", axis=0, tiled=True)
    group_rows = attention_rows.shape[0]
    seq_count = segments.shape[0]
    seq_length = segments.shape[1]
    token_positions = doc_positions(segments)
    local_queries = query_full.shape[1] // HEAD_SIZE
    local_keys = key_full.shape[1] // HEAD_SIZE
    each_group = local_queries // local_keys
    query_unnormed = jnp.dot(
        attention_rows, query_full, preferred_element_type=jnp.float32
    ).reshape(seq_count, seq_length, local_queries, HEAD_SIZE)
    key_unnormed = jnp.dot(attention_rows, key_full, preferred_element_type=jnp.float32).reshape(
        seq_count, seq_length, local_keys, HEAD_SIZE
    )
    value_rows = (
        jnp.dot(attention_rows, value_full, preferred_element_type=jnp.float32)
        .astype(jnp.bfloat16)
        .reshape(seq_count, seq_length, local_keys, HEAD_SIZE)
    )
    query_rows = (
        head_lookup(query_unnormed, query_norm_gain, token_positions)
        .astype(jnp.bfloat16)
        .reshape(seq_count, seq_length, local_keys, each_group, HEAD_SIZE)
    )
    keys = head_lookup(key_unnormed, key_gain, token_positions).astype(jnp.bfloat16)
    attended, log_total = lax.map(forward_item, (query_rows, keys, value_rows, segments))
    attended_flat = attended.reshape(group_rows, local_queries * HEAD_SIZE)
    mid = input_float + lax.psum_scatter(
        jnp.dot(attended_flat, output_full, preferred_element_type=jnp.float32),
        "tp",
        scatter_dimension=0,
        tiled=True,
    )
    hidden_in = rms_scale(mid, hidden_gain).astype(jnp.bfloat16)
    hidden_rows = lax.all_gather(hidden_in, "tp", axis=0, tiled=True)
    gate_value = jnp.dot(hidden_rows, gate_full, preferred_element_type=jnp.float32)
    up_value = jnp.dot(hidden_rows, up_full, preferred_element_type=jnp.float32)
    hidden = (jax.nn.silu(gate_value) * up_value).astype(jnp.bfloat16)
    layer_output = (
        mid
        + lax.psum_scatter(
            jnp.dot(hidden, down_full, preferred_element_type=jnp.float32).astype(jnp.bfloat16),
            "tp",
            scatter_dimension=0,
            tiled=True,
        ).astype(jnp.float32)
    ).astype(jnp.bfloat16)
    query_again, key_again, value_again, output_again = (
        lax.all_gather(query_weight, "fsdp", axis=0, tiled=True),
        lax.all_gather(key_matrix, "fsdp", axis=0, tiled=True),
        lax.all_gather(value_matrix, "fsdp", axis=0, tiled=True),
        lax.all_gather(output_matrix, "fsdp", axis=1, tiled=True),
    )
    gate_again, up_again, down_again = (
        lax.all_gather(gate_weight, "fsdp", axis=0, tiled=True),
        lax.all_gather(up_weight, "fsdp", axis=0, tiled=True),
        lax.all_gather(down_weight, "fsdp", axis=1, tiled=True),
    )
    cotangent_rows = lax.all_gather(cotangent, "tp", axis=0, tiled=True)
    hidden_back = contract_product(cotangent_rows, down_again, 1, 1)
    sigmoid = jax.nn.sigmoid(gate_value)
    gate_back = (hidden_back * up_value * sigmoid * (1.0 + gate_value * (1.0 - sigmoid))).astype(
        jnp.bfloat16
    )
    upward_back = (hidden_back * gate_value * sigmoid).astype(jnp.bfloat16)
    down_part = contract_product(hidden, cotangent_rows, 0, 0)
    gate_part = contract_product(hidden_rows, gate_back, 0, 0)
    up_part = contract_product(hidden_rows, upward_back, 0, 0)
    hidden_in_back = lax.psum_scatter(
        contract_product(gate_back, gate_again, 1, 1)
        + contract_product(upward_back, up_again, 1, 1),
        "tp",
        scatter_dimension=0,
        tiled=True,
    )
    mid_part, hidden_gain_part = jax.vjp(rms_scale, mid, hidden_gain)[1](hidden_in_back)
    mid_back = cotangent.astype(jnp.float32) + mid_part
    mixer_gradient = mid_back.astype(jnp.bfloat16)
    mixer_rows = lax.all_gather(mixer_gradient, "tp", axis=0, tiled=True)
    output_part = contract_product(attended_flat, mixer_rows, 0, 0)
    attended_gradient = (
        contract_product(mixer_rows, output_again, 1, 1)
        .astype(jnp.bfloat16)
        .reshape(seq_count, seq_length, local_keys, each_group, HEAD_SIZE)
    )
    query_back, key_back, value_gradient = lax.map(
        backward_item,
        (query_rows, keys, value_rows, segments, log_total, attended, attended_gradient),
    )
    query_back = query_back.reshape(seq_count, seq_length, local_queries, HEAD_SIZE)
    query_raw_back, query_gain_part = jax.vjp(
        partial(head_lookup, token_positions=token_positions), query_unnormed, query_norm_gain
    )[1](query_back)
    key_unnormed_gradient, key_gain_part = jax.vjp(
        partial(head_lookup, token_positions=token_positions), key_unnormed, key_gain
    )[1](key_back)
    query_low = query_raw_back.astype(jnp.bfloat16).reshape(group_rows, local_queries * HEAD_SIZE)
    key_reduced = key_unnormed_gradient.astype(jnp.bfloat16).reshape(
        group_rows, local_keys * HEAD_SIZE
    )
    value_reduced = value_gradient.reshape(group_rows, local_keys * HEAD_SIZE)
    query_part = contract_product(attention_rows, query_low, 0, 0)
    key_part = contract_product(attention_rows, key_reduced, 0, 0)
    value_part = contract_product(attention_rows, value_reduced, 0, 0)
    first_term = contract_product(query_low, query_again, 1, 1)
    second_term = contract_product(key_reduced, key_again, 1, 1)
    third_term = contract_product(value_reduced, value_again, 1, 1)
    attention_in_back = lax.psum_scatter(
        first_term + second_term + third_term, "tp", scatter_dimension=0, tiled=True
    )
    input_part, attention_gain_part = jax.vjp(rms_scale, input_float, attention_gain)[1](
        attention_in_back
    )
    input_gradient = (mid_back + input_part).astype(jnp.bfloat16)
    query_sum, key_sum, value_sum, output_sum, gate_sum, up_sum, down_sum = (
        lax.psum_scatter(query_part, "fsdp", scatter_dimension=0, tiled=True),
        lax.psum_scatter(key_part, "fsdp", scatter_dimension=0, tiled=True),
        lax.psum_scatter(value_part, "fsdp", scatter_dimension=0, tiled=True),
        lax.psum_scatter(output_part, "fsdp", scatter_dimension=1, tiled=True),
        lax.psum_scatter(gate_part, "fsdp", scatter_dimension=0, tiled=True),
        lax.psum_scatter(up_part, "fsdp", scatter_dimension=0, tiled=True),
        lax.psum_scatter(down_part, "fsdp", scatter_dimension=1, tiled=True),
    )
    gain_sums = lax.psum(
        (attention_gain_part, query_gain_part, key_gain_part, hidden_gain_part), ("fsdp", "tp")
    )
    return (
        layer_output,
        input_gradient,
        gain_sums[0],
        query_sum,
        key_sum,
        value_sum,
        gain_sums[1],
        gain_sums[2],
        output_sum,
        gain_sums[3],
        gate_sum,
        up_sum,
        down_sum,
    )


def solution(mesh):
    in_specs = (
        P(("fsdp", "tp"), None),
        P("fsdp", None),
        P(("fsdp", "tp"), None),
        P(),
        P("fsdp", "tp"),
        P("fsdp", "tp"),
        P("fsdp", "tp"),
        P(),
        P(),
        P("tp", "fsdp"),
        P(),
        P("fsdp", "tp"),
        P("fsdp", "tp"),
        P("tp", "fsdp"),
    )
    out_specs = (
        P(("fsdp", "tp"), None),
        P(("fsdp", "tp"), None),
        P(),
        P("fsdp", "tp"),
        P("fsdp", "tp"),
        P("fsdp", "tp"),
        P(),
        P(),
        P("tp", "fsdp"),
        P(),
        P("fsdp", "tp"),
        P("fsdp", "tp"),
        P("tp", "fsdp"),
    )
    return jax.shard_map(shards, mesh=mesh, in_specs=in_specs, out_specs=out_specs, check_vma=False)
```

profile of v0, /device:TPU:0, one launch (start us, length us, event | category | flops | bytes accessed | tf_op | source)
XLA Modules:
  0.0 1730.1 jit_solution(2496854354055952176)
XLA Ops:
  19.5 16.5 all-gather.16.cloned.1.call-done
  36.0 82.9 %all-gather.12.cloned.1.call-done = bf16[1024,2048]{1,0:T(8,128)(2,1)} async-done(((bf16[256,2048]{1,0:T(8,128)(2,1)}), bf16[1024,2048]{1,0:T(8,128)(2,1)}) %all-gather.12.cloned.1.call-update) | async-done | bytes 4194320 | tf_op jit(solution)/shard_map/all_gather | solution.py:156
  125.7 21.4 %all-gather.18.cloned.1.call-done = bf16[2048,512]{1,0:T(8,128)(2,1)} async-done(((bf16[256,512]{1,0:T(8,128)(2,1)}), bf16[2048,512]{1,0:T(8,128)(2,1)}) %all-gather.18.cloned.1.call-update) | async-done | bytes 2097168 | tf_op jit(solution)/shard_map/all_gather | solution.py:146
  178.3 17.6 %while.26 = (s32[]{:T(128)}, bf16[2,512,2,2,128]{4,3,2,1,0:T(2,128)(2,1)}, f32[2,2,2,512]{3,2,1,0:T(2,128)S(1)}, bf16[2,512,2,128]{3,2,1,0:T(2,128)(2,1)S(1)}, s...) while((s32[]{:T(128)}, ...), condition=%wide.region_7.8_spmd, body=%wide.region_5.7_spmd.sunk | while | flops 545257472 | bytes 13950561 | solution.py:181
  210.6 144.0 %reduce-scatter.12.cloned.1.call-done = f32[256,2048]{1,0:T(8,128)} async-done(((f32[1024,2048]{1,0:T(8,128)}), f32[256,2048]{1,0:T(8,128)}) %reduce-scatter.12.cloned.1.call-update) | async-done | bytes 2097168 | tf_op jit(solution)/shard_map/reduce_scatter | solution.py:183
  360.3 42.1 %all-gather.24.cloned.1.call-done = bf16[2048,1536]{1,0:T(8,128)(2,1)} async-done(((bf16[256,1536]{1,0:T(8,128)(2,1)}), bf16[2048,1536]{1,0:T(8,128)(2,1)}) %all-gather.24.cloned.1.call-update) | async-done | bytes 6291472 | tf_op jit(solution)/shard_map/all_gather | solution.py:152
  402.4 82.9 %all-gather.22.cloned.1.call-done = bf16[1024,2048]{1,0:T(8,128)(2,1)} async-done(((bf16[256,2048]{1,0:T(8,128)(2,1)}), bf16[1024,2048]{1,0:T(8,128)(2,1)}) %all-gather.22.cloned.1.call-update) | async-done | bytes 4194320 | tf_op jit(solution)/shard_map/all_gather | solution.py:190
  497.1 34.1 %all-gather.26.cloned.1.call-done = bf16[2048,1536]{1,0:T(8,128)(2,1)} async-done(((bf16[256,1536]{1,0:T(8,128)(2,1)}), bf16[2048,1536]{1,0:T(8,128)(2,1)}) %all-gather.26.cloned.1.call-update) | async-done | bytes 6291472 | tf_op jit(solution)/shard_map/all_gather | solution.py:153
  542.8 70.5 %all-gather.30.cloned.1.call-done = bf16[1024,2048]{1,0:T(8,128)(2,1)} async-done(((bf16[256,2048]{1,0:T(8,128)(2,1)}), bf16[1024,2048]{1,0:T(8,128)(2,1)}) %all-gather.30.cloned.1.call-update) | async-done | bytes 4194320 | tf_op jit(solution)/shard_map/all_gather | solution.py:214
  613.3 47.0 %all-gather.28.cloned.1.call-done = bf16[1536,2048]{1,0:T(8,128)(2,1)} async-done(((bf16[1536,256]{1,0:T(8,128)(2,1)}), bf16[1536,2048]{1,0:T(8,128)(2,1)}) %all-gather.28.cloned.1.call-update) | async-done | bytes 6291472 | tf_op jit(solution)/shard_map/all_gather | solution.py:154
  686.7 22.6 %convolution_add_fusion = f32[1024,2048]{1,0:T(8,128)} fusion(f32[1024,2048]{1,0:T(8,128)S(1)} %fusion.108, bf16[1024,1536]{1,0:T(8,128)(2,1)} %get-tuple-element.277, bf16[2048,1536]{1,0:T(8,128)(2,1)S(1)} %copy-done.58), kind=kOutput, calls=%fused_computation.86 | convolution fusion | flops 6444548096 | bytes 26214400 | tf_op jit(solution)/shard_map/dot_general | solution.py:56
  709.4 144.7 %reduce-scatter.16.cloned.1.call-done = f32[256,2048]{1,0:T(8,128)} async-done(((f32[1024,2048]{1,0:T(8,128)}), f32[256,2048]{1,0:T(8,128)}) %reduce-scatter.16.cloned.1.call-update) | async-done | bytes 2097168 | tf_op jit(solution)/shard_map/reduce_scatter | solution.py:224
  858.9 81.4 %all-gather.32.cloned.1.call-done = bf16[1024,2048]{1,0:T(8,128)(2,1)} async-done(((bf16[256,2048]{1,0:T(8,128)(2,1)}), bf16[1024,2048]{1,0:T(8,128)(2,1)}) %all-gather.32.cloned.1.call-update) | async-done | bytes 4194320 | tf_op jit(solution)/shard_map/all_gather | solution.py:234
  946.7 29.9 %while.27 = (s32[]{:T(128)}, f32[2,512,2,2,128]{1,4,3,2,0:T(8,128)}, f32[2,512,2,128]{1,3,2,0:T(8,128)}, bf16[2,512,2,128]{3,2,1,0:T(2,128)(2,1)}, bf16[2,512,2,...) while((s32[]{:T(128)}, ...), condition=%wide.region_14.15_spmd, body=%wide.region_13.14_spmd.sunk | while | flops 1355020288 | bytes 76359472 | solution.py:241
  1083.9 69.7 %reduce-scatter.18.cloned.1.call-done = f32[256,2048]{1,0:T(8,128)} async-done(((f32[1024,2048]{1,0:T(8,128)}), f32[256,2048]{1,0:T(8,128)}) %reduce-scatter.18.cloned.1.call-update) | async-done | bytes 2097168 | tf_op jit(solution)/shard_map/reduce_scatter | solution.py:263
  1155.8 46.1 %all-reduce.5 = (f32[2048]{0:T(1024)}, f32[128]{0:T(128)}, f32[128]{0:T(128)}, f32[2048]{0:T(1024)}) all-reduce(f32[2048]{0:T(1024)S(1)} %get-tuple-element.227, f32[128]{0:T(128)S(1)} %get-tuple-element.223, f32[128]{0:T(128)S(1)} %get-tuple-element.229, f32[2048]{0:T(1024)S(1)} %copy-done.45), channel_id=1, replica_groups=mesh['fsdp'=8,'tp'=4] {'fsdp','tp'}, use_global_device_ids=true, to_apply=%region_20.21 | all-reduce | flops 4352 | bytes 34816 | tf_op jit(solution)/shard_map/psum | solution.py:279
  1201.9 32.2 %reduce-scatter.14.cloned.1.call-done = bf16[256,2048]{1,0:T(8,128)(2,1)} async-done(((bf16[1024,2048]{1,0:T(8,128)(2,1)}), bf16[256,2048]{1,0:T(8,128)(2,1)}) %reduce-scatter.14.cloned.1.call-update) | async-done | bytes 1048592 | tf_op jit(solution)/shard_map/reduce_scatter | solution.py:196
  1239.4 91.5 %reduce-scatter.28.cloned.1.call-done = f32[256,1536]{1,0:T(8,128)} async-done(((f32[2048,1536]{1,0:T(8,128)}), f32[256,1536]{1,0:T(8,128)}) %reduce-scatter.28.cloned.1.call-update) | async-done | bytes 1572880 | tf_op jit(solution)/shard_map/reduce_scatter | solution.py:275
  1330.9 96.2 %reduce-scatter.30.cloned.1.call-done = f32[256,1536]{1,0:T(8,128)} async-done(((f32[2048,1536]{1,0:T(8,128)}), f32[256,1536]{1,0:T(8,128)}) %reduce-scatter.30.cloned.1.call-update) | async-done | bytes 1572880 | tf_op jit(solution)/shard_map/reduce_scatter | solution.py:276
  1427.1 95.9 %reduce-scatter.32.cloned.1.call-done = f32[1536,256]{1,0:T(8,128)} async-done(((f32[1536,2048]{1,0:T(8,128)}), f32[1536,256]{1,0:T(8,128)}) %reduce-scatter.32.cloned.1.call-update) | async-done | bytes 1572880 | tf_op jit(solution)/shard_map/reduce_scatter | solution.py:277
  1523.0 45.0 %reduce-scatter.22.cloned.1.call-done = f32[256,256]{1,0:T(8,128)} async-done(((f32[2048,256]{1,0:T(8,128)}), f32[256,256]{1,0:T(8,128)}) %reduce-scatter.22.cloned.1.call-update) | async-done | bytes 262160 | tf_op jit(solution)/shard_map/reduce_scatter | solution.py:272
  1568.0 44.9 %reduce-scatter.24.cloned.1.call-done = f32[256,256]{1,0:T(8,128)} async-done(((f32[2048,256]{1,0:T(8,128)}), f32[256,256]{1,0:T(8,128)}) %reduce-scatter.24.cloned.1.call-update) | async-done | bytes 262160 | tf_op jit(solution)/shard_map/reduce_scatter | solution.py:273
  1612.9 55.1 %reduce-scatter.26.cloned.1.call-done = f32[512,256]{1,0:T(8,128)} async-done(((f32[512,2048]{1,0:T(8,128)}), f32[512,256]{1,0:T(8,128)}) %reduce-scatter.26.cloned.1.call-update) | async-done | bytes 524304 | tf_op jit(solution)/shard_map/reduce_scatter | solution.py:274
  1667.9 55.1 %reduce-scatter.20.cloned.1.call-done = f32[256,512]{1,0:T(8,128)} async-done(((f32[2048,512]{1,0:T(8,128)}), f32[256,512]{1,0:T(8,128)}) %reduce-scatter.20.cloned.1.call-update) | async-done | bytes 524304 | tf_op jit(solution)/shard_map/reduce_scatter | solution.py:271
  (313 shorter events, 292.4 us)
Async XLA Ops:
  7.2 28.8 %all-gather.16.cloned.1.call-start = ((), (), s32[]{:S(2)}) async-start(), calls=%async_computation.13 | async-start | bytes 1179648 | tf_op jit(solution)/shard_map/all_gather | solution.py:147
  7.9 111.0 %all-gather.12.cloned.1.call-start = ((), (), s32[]{:S(2)}) async-start(), calls=%async_computation.11 | async-start | bytes 5242880 | tf_op jit(solution)/shard_map/all_gather | solution.py:156
  13.2 133.9 %all-gather.18.cloned.1.call-start = ((), (), s32[]{:S(2)}) async-start(), calls=%async_computation.14 | async-start | bytes 2359296 | tf_op jit(solution)/shard_map/all_gather | solution.py:146
  13.9 158.3 %all-gather.14.cloned.1.call-start = ((), (), s32[]{:S(2)}) async-start(), calls=%async_computation.12 | async-start | bytes 1179648 | tf_op jit(solution)/shard_map/all_gather | solution.py:148
  14.5 187.7 %all-gather.20.cloned.1.call-start = ((), (), s32[]{:S(2)}) async-start(), calls=%async_computation.15 | async-start | bytes 2359296 | tf_op jit(solution)/shard_map/all_gather | solution.py:149
  15.1 339.4 %reduce-scatter.12.cloned.1.call-start = ((), (), s32[]{:S(2)}) async-start(), calls=%async_computation.16 | async-start | bytes 10485760 | tf_op jit(solution)/shard_map/reduce_scatter | solution.py:183
  209.8 192.7 %all-gather.24.cloned.1.call-start = ((), (), s32[]{:S(2)}) async-start(), calls=%async_computation.18 | async-start | bytes 7077888 | tf_op jit(solution)/shard_map/all_gather | solution.py:152
  210.5 274.8 %all-gather.22.cloned.1.call-start = ((), (), s32[]{:S(2)}) async-start(), calls=%async_computation.17 | async-start | bytes 5242880 | tf_op jit(solution)/shard_map/all_gather | solution.py:190
  356.7 500.2 %copy-start.1 = (f32[256,2048]{1,0:T(8,128)}, f32[256,2048]{1,0:T(8,128)S(1)}, u32[]{:S(2)}) copy-start(f32[256,2048]{1,0:T(8,128)S(1)} %get-tuple-element.272) | copy-start | bytes 6291460
  356.7 500.2 %copy-start.46 = (f32[256]{0:T(256)}, f32[256]{0:T(256)S(1)}, u32[]{:S(2)}) copy-start(f32[256]{0:T(256)S(1)} %fusion.100) | copy-start | bytes 3076
  358.2 172.9 %all-gather.26.cloned.1.call-start = ((), (), s32[]{:S(2)}) async-start(), calls=%async_computation.19 | async-start | bytes 7077888 | tf_op jit(solution)/shard_map/all_gather | solution.py:153
  359.0 254.4 %all-gather.30.cloned.1.call-start = ((), (), s32[]{:S(2)}) async-start(), calls=%async_computation.22 | async-start | bytes 5242880 | tf_op jit(solution)/shard_map/all_gather | solution.py:214
  359.6 300.8 %all-gather.28.cloned.1.call-start = ((), (), s32[]{:S(2)}) async-start(), calls=%async_computation.20 | async-start | bytes 7077888 | tf_op jit(solution)/shard_map/all_gather | solution.py:154
  360.3 493.8 %reduce-scatter.16.cloned.1.call-start = ((), (), s32[]{:S(2)}) async-start(), calls=%async_computation.23 | async-start | bytes 10485760 | tf_op jit(solution)/shard_map/reduce_scatter | solution.py:224
  709.3 231.0 %all-gather.32.cloned.1.call-start = ((), (), s32[]{:S(2)}) async-start(), calls=%async_computation.24 | async-start | bytes 5242880 | tf_op jit(solution)/shard_map/all_gather | solution.py:234
  858.8 294.7 %reduce-scatter.18.cloned.1.call-start = ((), (), s32[]{:S(2)}) async-start(), calls=%async_computation.25 | async-start | bytes 10485760 | tf_op jit(solution)/shard_map/reduce_scatter | solution.py:263
  1010.3 223.9 %reduce-scatter.14.cloned.1.call-start = ((), (), s32[]{:S(2)}) async-start(), calls=%async_computation.21 | async-start | bytes 5242880 | tf_op jit(solution)/shard_map/reduce_scatter | solution.py:196
  1021.5 309.4 %reduce-scatter.28.cloned.1.call-start = ((), (), s32[]{:S(2)}) async-start(), calls=%async_computation.30 | async-start | bytes 14155776 | tf_op jit(solution)/shard_map/reduce_scatter | solution.py:275
  1034.0 393.1 %reduce-scatter.30.cloned.1.call-start = ((), (), s32[]{:S(2)}) async-start(), calls=%async_computation.31 | async-start | bytes 14155776 | tf_op jit(solution)/shard_map/reduce_scatter | solution.py:276
  1046.9 476.2 %reduce-scatter.32.cloned.1.call-start = ((), (), s32[]{:S(2)}) async-start(), calls=%async_computation.32 | async-start | bytes 14155776 | tf_op jit(solution)/shard_map/reduce_scatter | solution.py:277
  1059.3 508.7 %reduce-scatter.22.cloned.1.call-start = ((), (), s32[]{:S(2)}) async-start(), calls=%async_computation.27 | async-start | bytes 2359296 | tf_op jit(solution)/shard_map/reduce_scatter | solution.py:272
  1064.3 548.6 %reduce-scatter.24.cloned.1.call-start = ((), (), s32[]{:S(2)}) async-start(), calls=%async_computation.28 | async-start | bytes 2359296 | tf_op jit(solution)/shard_map/reduce_scatter | solution.py:273
  1069.2 598.7 %reduce-scatter.26.cloned.1.call-start = ((), (), s32[]{:S(2)}) async-start(), calls=%async_computation.29 | async-start | bytes 4718592 | tf_op jit(solution)/shard_map/reduce_scatter | solution.py:274
  1076.0 647.1 %reduce-scatter.20.cloned.1.call-start = ((), (), s32[]{:S(2)}) async-start(), calls=%async_computation.26 | async-start | bytes 4718592 | tf_op jit(solution)/shard_map/reduce_scatter | solution.py:271
  (65 other events, 1849.8 us)
Sparse Core Ops, SparseCore 0:
  9.9 26.0 all-gather.15
  38.2 80.7 all-gather.11
  120.8 26.2 all-gather.17
  148.9 23.3 all-gather.13
  174.0 28.1 all-gather.19
  209.9 144.6 reduce-scatter.11
  356.4 45.9 all-gather.23
  404.6 80.7 all-gather.21
  487.2 43.8 all-gather.25
  532.6 80.7 all-gather.29
  615.2 45.0 all-gather.27
  709.5 144.6 reduce-scatter.15
  858.9 81.3 all-gather.31
  1010.4 143.0 reduce-scatter.17
  1155.7 78.4 reduce-scatter.13
  1238.1 92.7 reduce-scatter.27
  1334.8 92.2 reduce-scatter.29
  1431.0 91.9 reduce-scatter.31
  1526.9 41.1 reduce-scatter.21
  1571.7 41.1 reduce-scatter.23
  1616.8 51.0 reduce-scatter.25
  1671.9 51.1 reduce-scatter.19
where the time goes:
time: 1730 us
  waiting for transfers between devices  1370 us (79%)
  matrix products  206 us (12%)
  other arithmetic  55.3 us (3%)
  blocking collectives  46.1 us (3%)
  local copies, waits for them, and re-layouts  40.1 us (2%)
    reduce_scatter x1, waiting for transfers between devices, shards(): lax.psum_scatter(contract_product(gate_back, gate_again, 1, 1) + contract...  145 us
    reduce_scatter x1, waiting for transfers between devices, shards(): lax.psum_scatter(jnp.dot(attended_flat, output_full, preferred_element_ty...  144 us
    dot_general x14, matrix products, contract_product(): lax.dot_general(left_side, right_side, (((left_dim,), (right_dim,)), ((),...  123 us
    reduce_scatter x1, waiting for transfers between devices, shards(): lax.psum_scatter(up_part, 'fsdp', scatter_dimension=0, tiled=True)  96.2 us
    reduce_scatter x1, waiting for transfers between devices, shards(): lax.psum_scatter(down_part, 'fsdp', scatter_dimension=1, tiled=True)  95.9 us
    reduce_scatter x1, waiting for transfers between devices, shards(): lax.psum_scatter(gate_part, 'fsdp', scatter_dimension=0, tiled=True)  91.5 us
    all_gather x1, waiting for transfers between devices, shards(): attention_rows = lax.all_gather(attention_input, 'tp', axis=0, tiled=True)  82.9 us
    all_gather x1, waiting for transfers between devices, shards(): hidden_rows = lax.all_gather(hidden_in, 'tp', axis=0, tiled=True)  82.9 us
  transfers between devices with their start and end apart: 22, of which 22 were waited for; matrix products, arithmetic and copies ran while one was open for 10% of the time, Pallas kernels for 0%

commit v1 on v0

v1 whole, which is shorter than its diff:
```python
import math
from functools import partial

import jax
import jax.numpy as jnp
from jax import lax
from jax.sharding import PartitionSpec as P

EPSILON = 1e-06
THETA = 1000000.0


def rms_scale(value_rows, norm_gain):
    return (
        value_rows
        * lax.rsqrt(jnp.mean(value_rows * value_rows, axis=-1, keepdims=True) + EPSILON)
        * norm_gain
    )


def doc_positions(segments):
    length = segments.shape[-1]
    indices = jnp.arange(length, dtype=jnp.int32)
    leading = jnp.ones(segments.shape[:-1] + (1,), dtype=jnp.bool_)
    change = jnp.concatenate([leading, segments[..., 1:] != segments[..., :-1]], axis=-1)
    starts = lax.cummax(jnp.where(change, indices, jnp.int32(0)), axis=segments.ndim - 1)
    return indices - starts


def rotate(vectors, cosine_table, sine_table):
    half_dim = vectors.shape[-1] // 2
    first_half = vectors[..., :half_dim]
    second_half = vectors[..., half_dim:]
    return jnp.concatenate(
        [
            first_half * cosine_table - second_half * sine_table,
            second_half * cosine_table + first_half * sine_table,
        ],
        axis=-1,
    )


def head_lookup(raw_heads, norm_gain, cosine_table, sine_table):
    return rotate(rms_scale(raw_heads, norm_gain), cosine_table, sine_table)


def contract(left_side, right_side, left_dim, right_dim):
    return lax.dot_general(
        left_side,
        right_side,
        (((left_dim,), (right_dim,)), ((), ())),
        preferred_element_type=jnp.float32,
    )


def attend_forward(query_rows, keys, value_rows, allowed):
    score_scale = 1.0 / math.sqrt(query_rows.shape[-1])
    scores = (
        jnp.einsum("qkgd,ckd->kgqc", query_rows, keys, preferred_element_type=jnp.float32)
        * score_scale
    )
    exponent = jnp.where(allowed, jnp.exp(scores), 0.0)
    log_total = jnp.log(jnp.sum(exponent, axis=-1))
    probability = jnp.where(allowed, jnp.exp(scores - log_total[..., None]), 0.0).astype(
        jnp.bfloat16
    )
    attended = jnp.einsum(
        "kgqc,ckd->qkgd", probability, value_rows, preferred_element_type=jnp.float32
    ).astype(jnp.bfloat16)
    return (attended, log_total)


def attend_backward(query_rows, keys, value_rows, allowed, log_total, attended, attended_gradient):
    score_scale = 1.0 / math.sqrt(query_rows.shape[-1])
    scores = (
        jnp.einsum("qkgd,ckd->kgqc", query_rows, keys, preferred_element_type=jnp.float32)
        * score_scale
    )
    probability = jnp.where(allowed, jnp.exp(scores - log_total[..., None]), 0.0)
    prob_low = probability.astype(jnp.bfloat16)
    delta = jnp.einsum(
        "qkgd,qkgd->kgq", attended_gradient, attended, preferred_element_type=jnp.float32
    )
    value_dots = jnp.einsum(
        "qkgd,ckd->kgqc", attended_gradient, value_rows, preferred_element_type=jnp.float32
    )
    score_back = (probability * (value_dots - delta[..., None])).astype(jnp.bfloat16)
    query_back = (
        jnp.einsum("kgqc,ckd->qkgd", score_back, keys, preferred_element_type=jnp.float32)
        * score_scale
    )
    key_back = (
        jnp.einsum("kgqc,qkgd->ckd", score_back, query_rows, preferred_element_type=jnp.float32)
        * score_scale
    )
    value_gradient = jnp.einsum(
        "kgqc,qkgd->ckd", prob_low, attended_gradient, preferred_element_type=jnp.float32
    ).astype(jnp.bfloat16)
    return (query_back, key_back, value_gradient)


def shards(
    sizes,
    layer_input,
    segments,
    cotangent,
    attention_gain,
    query_weight,
    key_matrix,
    value_matrix,
    query_norm_gain,
    key_gain,
    output_matrix,
    hidden_gain,
    gate_weight,
    up_weight,
    down_weight,
):
    fsdp, tp = sizes
    low = jnp.bfloat16
    own_rows, width = layer_input.shape
    seq_count, seq_length = segments.shape
    head_size = query_norm_gain.shape[0]
    team = tp // seq_count
    sets = seq_count
    me = lax.axis_index("tp")
    place = me % team

    def hop(value, step):
        return lax.ppermute(value, "tp", [(i, (i + step) % tp) for i in range(tp)])

    def team_hop(value, step):
        return lax.ppermute(
            value, "tp", [(i, i // team * team + (i + step) % team) for i in range(tp)]
        )

    def team_rows(own):
        return jnp.concatenate([own] + [team_hop(own, step) for step in range(1, team)], axis=0)

    def team_sum(partial_rows):
        total = partial_rows[:own_rows]
        for step in range(1, team):
            block = partial_rows[step * own_rows : (step + 1) * own_rows].astype(low)
            total = total + team_hop(block, team - step).astype(jnp.float32)
        return total

    def ring_rows(own):
        blocks = [own]
        for _ in range(1, tp):
            blocks.append(hop(blocks[-1], 1))
        return blocks

    def ring_sum(blocks):
        carried = blocks[1]
        for step in range(2, tp + 1):
            carried = hop(carried.astype(low), 1).astype(jnp.float32) + blocks[step % tp]
        return carried

    input_float = layer_input.astype(jnp.float32)
    attention_input = rms_scale(input_float, attention_gain).astype(low)
    attention_rows = team_rows(attention_input)

    own_set = jnp.concatenate(
        [query_weight, key_matrix, value_matrix, output_matrix.T], axis=1
    )
    weight_sets = [own_set] + [
        lax.ppermute(
            own_set,
            "tp",
            [(i, (i // team + m) % sets * team + i % team) for i in range(tp)],
        )
        for m in range(1, sets)
    ]
    set_full = [lax.all_gather(w, "fsdp", axis=0, tiled=True) for w in weight_sets]
    gate_full = lax.all_gather(gate_weight, "fsdp", axis=0, tiled=True)
    up_full = lax.all_gather(up_weight, "fsdp", axis=0, tiled=True)
    down_full = lax.all_gather(down_weight, "fsdp", axis=1, tiled=True)

    query_width = query_weight.shape[1]
    key_width = key_matrix.shape[1]
    mix_width = query_width + 2 * key_width
    local_queries = query_width // head_size
    local_keys = key_width // head_size
    each_group = local_queries // local_keys

    own_segments = lax.dynamic_index_in_dim(segments, me // team, 0, keepdims=False)
    own_positions = doc_positions(own_segments)
    blocks = [
        (place + team - step) % team * own_rows + jnp.arange(own_rows, dtype=jnp.int32)
        for step in range(team)
    ]
    tokens = jnp.concatenate(blocks)
    row_segments = own_segments[tokens]
    row_positions = own_positions[tokens]
    allowed = (tokens[:, None] >= tokens[None, :]) & (
        row_segments[:, None] == row_segments[None, :]
    )
    exponents = jnp.arange(head_size // 2, dtype=jnp.float32) * (-2.0 / head_size)
    frequencies = jnp.power(jnp.float32(THETA), exponents)
    angles = row_positions.astype(jnp.float32)[:, None] * frequencies
    cosine_table = jnp.cos(angles)[:, None, :]
    sine_table = jnp.sin(angles)[:, None, :]

    saved = []
    mixed = None
    for full in set_full:
        raw = jnp.dot(attention_rows, full[:, :mix_width], preferred_element_type=jnp.float32)
        query_raw = raw[:, :query_width].reshape(seq_length, local_queries, head_size)
        key_raw = raw[:, query_width : query_width + key_width].reshape(
            seq_length, local_keys, head_size
        )
        value_rows = (
            raw[:, query_width + key_width :].astype(low).reshape(seq_length, local_keys, head_size)
        )
        query_rows = (
            head_lookup(query_raw, query_norm_gain, cosine_table, sine_table)
            .astype(low)
            .reshape(seq_length, local_keys, each_group, head_size)
        )
        keys = head_lookup(key_raw, key_gain, cosine_table, sine_table).astype(low)
        attended, log_total = attend_forward(query_rows, keys, value_rows, allowed)
        saved.append((query_raw, key_raw, query_rows, keys, value_rows, attended, log_total))
        attended_flat = attended.reshape(seq_length, query_width)
        term = contract(attended_flat, full[:, mix_width:], 1, 1)
        mixed = term if mixed is None else mixed + term

    mid = input_float + team_sum(mixed)
    hidden_in = rms_scale(mid, hidden_gain).astype(low)

    cotangent_blocks = ring_rows(cotangent)
    hidden_blocks = ring_rows(hidden_in)
    out_parts, in_parts, hiddens, gate_backs, up_backs = [], [], [], [], []
    for cotangent_rows, hidden_rows in zip(cotangent_blocks, hidden_blocks):
        gate_value = jnp.dot(hidden_rows, gate_full, preferred_element_type=jnp.float32)
        up_value = jnp.dot(hidden_rows, up_full, preferred_element_type=jnp.float32)
        hidden_back = contract(cotangent_rows, down_full, 1, 1)
        sigmoid = jax.nn.sigmoid(gate_value)
        hidden = (gate_value * sigmoid * up_value).astype(low)
        gate_back = (
            hidden_back * up_value * sigmoid * (1.0 + gate_value * (1.0 - sigmoid))
        ).astype(low)
        up_back = (hidden_back * gate_value * sigmoid).astype(low)
        hiddens.append(hidden)
        gate_backs.append(gate_back)
        up_backs.append(up_back)
        in_parts.append(contract(gate_back, gate_full, 1, 1) + contract(up_back, up_full, 1, 1))
        out_parts.append(jnp.dot(hidden, down_full, preferred_element_type=jnp.float32))

    hidden_in_back = ring_sum(in_parts)
    layer_output = (mid + ring_sum(out_parts)).astype(low)

    hidden_all = jnp.concatenate(hiddens, axis=0)
    gate_back_all = jnp.concatenate(gate_backs, axis=0)
    up_back_all = jnp.concatenate(up_backs, axis=0)
    hidden_in_all = jnp.concatenate(hidden_blocks, axis=0)
    cotangent_all = jnp.concatenate(cotangent_blocks, axis=0)

    def scatter(value, dim):
        return lax.psum_scatter(value.astype(low), "fsdp", scatter_dimension=dim, tiled=True)

    down_sum = scatter(contract(hidden_all, cotangent_all, 0, 0), 1).astype(jnp.float32)
    gate_sum = scatter(contract(hidden_in_all, gate_back_all, 0, 0), 0).astype(jnp.float32)
    up_sum = scatter(contract(hidden_in_all, up_back_all, 0, 0), 0).astype(jnp.float32)

    mid_part, hidden_gain_part = jax.vjp(rms_scale, mid, hidden_gain)[1](hidden_in_back)
    mid_back = cotangent.astype(jnp.float32) + mid_part
    mixer_rows = team_rows(mid_back.astype(low))

    lookup = partial(head_lookup, cosine_table=cosine_table, sine_table=sine_table)
    in_back = None
    query_gain_part = key_gain_part = 0.0
    mix_sums, output_sums = [], []
    for full, kept in zip(set_full, saved):
        query_raw, key_raw, query_rows, keys, value_rows, attended, log_total = kept
        attended_flat = attended.reshape(seq_length, query_width)
        output_sums.append(scatter(contract(mixer_rows, attended_flat, 0, 0), 0))
        attended_gradient = (
            jnp.dot(mixer_rows, full[:, mix_width:], preferred_element_type=jnp.float32)
            .astype(low)
            .reshape(seq_length, local_keys, each_group, head_size)
        )
        query_back, key_back, value_gradient = attend_backward(
            query_rows, keys, value_rows, allowed, log_total, attended, attended_gradient
        )
        query_back = query_back.reshape(seq_length, local_queries, head_size)
        query_raw_back, query_gain_add = jax.vjp(lookup, query_raw, query_norm_gain)[1](query_back)
        key_raw_back, key_gain_add = jax.vjp(lookup, key_raw, key_gain)[1](key_back)
        query_gain_part = query_gain_part + query_gain_add
        key_gain_part = key_gain_part + key_gain_add
        mix_low = jnp.concatenate(
            [
                query_raw_back.astype(low).reshape(seq_length, query_width),
                key_raw_back.astype(low).reshape(seq_length, key_width),
                value_gradient.reshape(seq_length, key_width),
            ],
            axis=1,
        )
        term = contract(mix_low, full[:, :mix_width], 1, 1)
        in_back = term if in_back is None else in_back + term
        mix_sums.append(scatter(contract(attention_rows, mix_low, 0, 0), 0))

    attention_in_back = team_sum(in_back)
    input_part, attention_gain_part = jax.vjp(rms_scale, input_float, attention_gain)[1](
        attention_in_back
    )
    input_gradient = (mid_back + input_part).astype(low)

    def home(parts):
        total = parts[0].astype(jnp.float32)
        for m in range(1, sets):
            moved = lax.ppermute(
                parts[m],
                "tp",
                [(i, (i // team + sets - m) % sets * team + i % team) for i in range(tp)],
            )
            total = total + moved.astype(jnp.float32)
        return total

    output_sum = home(output_sums).T
    mix_sum = home(mix_sums)
    query_sum = mix_sum[:, :query_width]
    key_sum = mix_sum[:, query_width : query_width + key_width]
    value_sum = mix_sum[:, query_width + key_width :]

    gains = jnp.concatenate(
        [attention_gain_part, hidden_gain_part, query_gain_part, key_gain_part]
    )
    for axis, size in (("fsdp", fsdp), ("tp", tp)):
        bit = 1
        while bit < size:
            gains = gains + lax.ppermute(gains, axis, [(i, i ^ bit) for i in range(size)])
            bit *= 2
    return (
        layer_output,
        input_gradient,
        gains[:width],
        query_sum,
        key_sum,
        value_sum,
        gains[2 * width : 2 * width + head_size],
        gains[2 * width + head_size :],
        output_sum,
        gains[width : 2 * width],
        gate_sum,
        up_sum,
        down_sum,
    )


def solution(mesh):
    rows = P(("fsdp", "tp"), None)
    in_specs = (
        rows,
        P("fsdp", None),
        rows,
        P(),
        P("fsdp", "tp"),
        P("fsdp", "tp"),
        P("fsdp", "tp"),
        P(),
        P(),
        P("tp", "fsdp"),
        P(),
        P("fsdp", "tp"),
        P("fsdp", "tp"),
        P("tp", "fsdp"),
    )
    out_specs = (
        rows,
        rows,
        P(),
        P("fsdp", "tp"),
        P("fsdp", "tp"),
        P("fsdp", "tp"),
        P(),
        P(),
        P("tp", "fsdp"),
        P(),
        P("fsdp", "tp"),
        P("fsdp", "tp"),
        P("tp", "fsdp"),
    )
    sizes = (mesh.shape["fsdp"], mesh.shape["tp"])
    return jax.shard_map(
        partial(shards, sizes),
        mesh=mesh,
        in_specs=in_specs,
        out_specs=out_specs,
        check_vma=False,
    )
```

time: 1730 us -> 915 us (0.53)
  waiting for transfers between devices: 1370 us -> 546 us
  blocking collectives: 46.1 us -> 0 us
  starting transfers between devices: 1.1 us -> 24.5 us
  local copies, waits for them, and re-layouts: 40.1 us -> 62.8 us
    reduce_scatter x11 -> x7, waiting for transfers between devices: 874 us -> 226 us  [scatter(): lax.psum_scatter(value.astype(low), 'fsdp', scatter_dimension=dim, tiled=...]
    all_gather x11 -> x5, waiting for transfers between devices: 486 us -> 45.6 us  [the longest x1 41.4 us: shards(): gate_full = lax.all_gather(gate_weight, 'fsdp', axis=0, tiled=True)]
    ppermute x0 -> x24, waiting for transfers between devices: none -> 273 us  [the longest x12 153 us: hop(): return lax.ppermute(value, 'tp', [(i, (i + step) % tp) for i in range(tp)])]
    psum x1 -> x0, blocking collectives: 46.1 us -> none  [shards(): lax.psum((attention_gain_part, query_gain_part, key_gain_part, hidden_gai...]
    ppermute x0 -> x24, starting transfers between devices: none -> 23.6 us  [the longest x12 11.1 us: hop(): return lax.ppermute(value, 'tp', [(i, (i + step) % tp) for i in range(tp)])]
    unnamed x112 -> x256, local copies, waits for them, and re-layouts: 7.12 us -> 25.3 us
    dot_general x22 -> x27, matrix products: 152 us -> 134 us  [the longest x23 117 us: contract(): lax.dot_general(left_side, right_side, (((left_dim,), (right_dim,)), ((),...]
  transfers between devices with their start and end apart: 22 -> 36, of which waited for: 22 -> 25; matrix products, arithmetic and copies ran while one was open for 10% -> 29% of each run, Pallas kernels for 0% -> 0%
where the time goes in v1:
time: 915 us; the launch traced here: 906 us
  waiting for transfers between devices  546 us (60%)
  matrix products  203 us (22%)
  local copies, waits for them, and re-layouts  62.8 us (7%)
  other arithmetic  52.6 us (6%)
  starting transfers between devices  24.5 us (3%)
  between operations  16.3 us (2%)
    reduce_scatter x7, waiting for transfers between devices, scatter(): lax.psum_scatter(value.astype(low), 'fsdp', scatter_dimension=dim, tiled=...  226 us
    ppermute x12, waiting for transfers between devices, hop(): return lax.ppermute(value, 'tp', [(i, (i + step) % tp) for i in range(tp)])  153 us
    dot_general x23, matrix products, contract(): lax.dot_general(left_side, right_side, (((left_dim,), (right_dim,)), ((),...  117 us
    ppermute x4, waiting for transfers between devices, team_hop(): lax.ppermute(value, 'tp', [(i, i // team * team + (i + step) % team) for...  62.9 us
    all_gather x1, waiting for transfers between devices, shards(): gate_full = lax.all_gather(gate_weight, 'fsdp', axis=0, tiled=True)  41.4 us
    ppermute x1, waiting for transfers between devices, shards(): lax.ppermute(own_set, 'tp', [(i, (i // team + m) % sets * team + i % team...  34.6 us
    unnamed x256, local copies, waits for them, and re-layouts  25.3 us
  transfers between devices with their start and end apart: 36, of which 25 were waited for; matrix products, arithmetic and copies ran while one was open for 29% of the time, Pallas kernels for 0%

profile of v1, /device:TPU:0, one launch (start us, length us, event | category | flops | bytes accessed | tf_op | source)
XLA Modules:
  0.0 905.7 jit_solution(17377006382564349314)
XLA Ops:
  16.4 34.6 %collective-permute-done.1 = bf16[256,1536]{0,1:T(8,128)(2,1)S(1)} collective-permute-done((bf16[256,1536]{0,1:T(8,128)(2,1)}, bf16[256,1536]{0,1:T(8,128)(2,1)S(1)}, u32[]{:S(2)}, u32[]{:S(2)}) %collective-permute-start.1) | collective-permute-done | bytes 786464 | tf_op jit(solution)/shard_map/ppermute | solution.py:167
  68.7 37.0 %collective-permute-done.9 = bf16[256,2048]{1,0:T(8,128)(2,1)} collective-permute-done((bf16[256,2048]{1,0:T(8,128)(2,1)S(1)}, bf16[256,2048]{1,0:T(8,128)(2,1)}, u32[]{:S(2)}, u32[]{:S(2)}) %collective-permute-start.9) | collective-permute-done | bytes 1048608 | tf_op jit(solution)/shard_map/ppermute | solution.py:130
  144.5 6.5 fusion.5
  158.7 6.2 fusion.3
  182.4 16.1 %collective-permute-done.2 = bf16[256,2048]{1,0:T(8,128)(2,1)} collective-permute-done((bf16[256,2048]{1,0:T(8,128)(2,1)S(1)}, bf16[256,2048]{1,0:T(8,128)(2,1)}, u32[]{:S(2)}, u32[]{:S(2)}) %collective-permute-start.2) | collective-permute-done | bytes 1048608 | tf_op jit(solution)/shard_map/ppermute | solution.py:133
  212.2 41.4 %all-gather.10.cloned.1.call-done = bf16[2048,1536]{1,0:T(8,128)(2,1)} async-done(((bf16[256,1536]{1,0:T(8,128)(2,1)}), bf16[2048,1536]{1,0:T(8,128)(2,1)}) %all-gather.10.cloned.1.call-update) | async-done | bytes 6291472 | tf_op jit(solution)/shard_map/all_gather | solution.py:175
  253.6 7.0 multiply_convert_fusion.1
  306.1 7.2 collective-permute-done.10
  315.1 20.6 %collective-permute-done.4 = bf16[256,2048]{1,0:T(8,128)(2,1)S(1)} collective-permute-done((bf16[256,2048]{1,0:T(8,128)(2,1)S(1)}, bf16[256,2048]{1,0:T(8,128)(2,1)S(1)}, u32[]{:S(2)}, u32[]{:S(2)}) %collective-permute-start.4) | collective-permute-done | bytes 1048608 | tf_op jit(solution)/shard_map/ppermute | solution.py:130
  338.0 20.2 %collective-permute-done.7 = bf16[256,2048]{1,0:T(8,128)(2,1)S(1)} collective-permute-done((bf16[256,2048]{1,0:T(8,128)(2,1)S(1)}, bf16[256,2048]{1,0:T(8,128)(2,1)S(1)}, u32[]{:S(2)}, u32[]{:S(2)}) %collective-permute-start.7) | collective-permute-done | bytes 1048608 | tf_op jit(solution)/shard_map/ppermute | solution.py:130
  382.9 20.3 %collective-permute-done.6 = bf16[256,2048]{1,0:T(8,128)(2,1)S(1)} collective-permute-done((bf16[256,2048]{1,0:T(8,128)(2,1)S(1)}, bf16[256,2048]{1,0:T(8,128)(2,1)S(1)}, u32[]{:S(2)}, u32[]{:S(2)}) %collective-permute-start.6) | collective-permute-done | bytes 1048608 | tf_op jit(solution)/shard_map/ppermute | solution.py:130
  405.5 20.1 %collective-permute-done.14 = bf16[256,2048]{1,0:T(8,128)(2,1)S(1)} collective-permute-done((bf16[256,2048]{1,0:T(8,128)(2,1)S(1)}, bf16[256,2048]{1,0:T(8,128)(2,1)S(1)}, u32[]{:S(2)}, u32[]{:S(2)}) %collective-permute-start.14) | collective-permute-done | bytes 1048608 | tf_op jit(solution)/shard_map/ppermute | solution.py:130
  428.0 19.4 %collective-permute-done.8 = bf16[256,2048]{1,0:T(8,128)(2,1)S(1)} collective-permute-done((bf16[256,2048]{1,0:T(8,128)(2,1)S(1)}, bf16[256,2048]{1,0:T(8,128)(2,1)S(1)}, u32[]{:S(2)}, u32[]{:S(2)}) %collective-permute-start.8) | collective-permute-done | bytes 1048608 | tf_op jit(solution)/shard_map/ppermute | solution.py:130
  450.4 24.4 %collective-permute-done.15 = bf16[256,2048]{1,0:T(8,128)(2,1)S(1)} collective-permute-done((bf16[256,2048]{1,0:T(8,128)(2,1)S(1)}, bf16[256,2048]{1,0:T(8,128)(2,1)S(1)}, u32[]{:S(2)}, u32[]{:S(2)}) %collective-permute-start.15) | collective-permute-done | bytes 1048608 | tf_op jit(solution)/shard_map/ppermute | solution.py:133
  527.3 6.9 fusion.95
  557.9 12.4 %convolution_convert_fusion.2 = bf16[2048,1536]{1,0:T(8,128)(2,1)} fusion(bf16[256,1536]{1,0:T(8,128)(2,1)} %copy-done.109, bf16[256,1536]{1,0:T(8,128)(2,1)} %copy-done.108, bf16[256,1536]{1,0:T(8,128)(2,1)} %copy-done.107, bf16[256,1536]{1,0:T(8,128)(2,1)} %copy-done.106, bf16[256,2048]{1,0:T(8,128)(2,1)} %copy-done.101, ...), kind=kOutput, calls=%fused_computation.6 | convolution fusion | flops 6474956800 | bytes 13631488 | tf_op jit(solution)/shard_map/dot_general | solution.py:48
  571.3 12.6 %convolution_convert_fusion.1 = bf16[2048,1536]{1,0:T(8,128)(2,1)} fusion(bf16[256,1536]{1,0:T(8,128)(2,1)} %copy-done.103, bf16[256,1536]{1,0:T(8,128)(2,1)} %copy-done.104, bf16[256,1536]{1,0:T(8,128)(2,1)} %copy-done.105, bf16[256,1536]{1,0:T(8,128)(2,1)S(1)} %copy-done.67, bf16[256,2048]{1,0:T(8,128)(2,1)} %copy-done.101, ...), kind=kOutput, calls=%fused_computation.5 | convolution fusion | flops 6474956800 | bytes 13631488 | tf_op jit(solution)/shard_map/dot_general | solution.py:48
  585.5 12.0 %convolution_convert_fusion = bf16[1536,2048]{1,0:T(8,128)(2,1)} fusion(bf16[256,2048]{1,0:T(8,128)(2,1)} %collective-permute-done.13, bf16[256,2048]{1,0:T(8,128)(2,1)} %collective-permute-done.11, bf16[256,2048]{1,0:T(8,128)(2,1)} %collective-permute-done.9, bf16[256,2048]{1,0:T(8,128)(2,1)S(1)} %copy-done.59, bf16[256,1536]{1,0:T(8,128)(2,1)} %copy-done.112, ...), kind=kOutput, calls=%fused_computation.4 | convolution fusion | flops 6474956800 | bytes 13631488 | tf_op jit(solution)/shard_map/dot_general | solution.py:48
  605.2 22.3 %collective-permute-done.16 = bf16[256,2048]{1,0:T(8,128)(2,1)S(1)} collective-permute-done((bf16[256,2048]{1,0:T(8,128)(2,1)S(1)}, bf16[256,2048]{1,0:T(8,128)(2,1)S(1)}, u32[]{:S(2)}, u32[]{:S(2)}) %collective-permute-start.16) | collective-permute-done | bytes 1048608 | tf_op jit(solution)/shard_map/ppermute | solution.py:133
  650.3 10.3 %collective-permute-done.23 = bf16[256,512]{1,0:T(8,128)(2,1)S(1)} collective-permute-done((bf16[256,512]{1,0:T(8,128)(2,1)}, bf16[256,512]{1,0:T(8,128)(2,1)S(1)}, u32[]{:S(2)}, u32[]{:S(2)}) %collective-permute-start.23) | collective-permute-done | bytes 262176 | tf_op jit(solution)/shard_map/ppermute | solution.py:311
  662.6 38.4 %reduce-scatter.8.cloned.1.call-done = bf16[256,1024]{1,0:T(8,128)(2,1)} async-done(((bf16[2048,1024]{1,0:T(8,128)(2,1)}), bf16[256,1024]{1,0:T(8,128)(2,1)}) %reduce-scatter.8.cloned.1.call-update) | async-done | bytes 524304 | tf_op jit(solution)/shard_map/reduce_scatter | solution.py:259
  703.9 62.1 %reduce-scatter.16.cloned.1.call-done = bf16[256,1536]{1,0:T(8,128)(2,1)} async-done(((bf16[2048,1536]{1,0:T(8,128)(2,1)}), bf16[256,1536]{1,0:T(8,128)(2,1)}) %reduce-scatter.16.cloned.1.call-update) | async-done | bytes 786448 | tf_op jit(solution)/shard_map/reduce_scatter | solution.py:259
  768.5 62.7 %reduce-scatter.18.cloned.1.call-done = bf16[256,1536]{1,0:T(8,128)(2,1)} async-done(((bf16[2048,1536]{1,0:T(8,128)(2,1)}), bf16[256,1536]{1,0:T(8,128)(2,1)}) %reduce-scatter.18.cloned.1.call-update) | async-done | bytes 786448 | tf_op jit(solution)/shard_map/reduce_scatter | solution.py:259
  833.7 62.4 %reduce-scatter.20.cloned.1.call-done = bf16[1536,256]{1,0:T(8,128)(2,1)} async-done(((bf16[1536,2048]{1,0:T(8,128)(2,1)}), bf16[1536,256]{1,0:T(8,128)(2,1)}) %reduce-scatter.20.cloned.1.call-update) | async-done | bytes 786448 | tf_op jit(solution)/shard_map/reduce_scatter | solution.py:259
  (478 shorter events, 306.0 us)
Async XLA Ops:
  7.2 98.5 %all-gather.6.cloned.1.call-start = ((), (), s32[]{:S(2)}) async-start(), calls=%async_computation.7 | async-start | bytes 7077888 | tf_op jit(solution)/shard_map/all_gather | solution.py:174
  12.2 106.4 %all-gather.8.cloned.1.call-start = ((), (), s32[]{:S(2)}) async-start(), calls=%async_computation.8 | async-start | bytes 7077888 | tf_op jit(solution)/shard_map/all_gather | solution.py:174
  51.9 124.5 %all-gather.14.cloned.1.call-start = ((), (), s32[]{:S(2)}) async-start(), calls=%async_computation.11 | async-start | bytes 7077888 | tf_op jit(solution)/shard_map/all_gather | solution.py:177
  52.7 153.8 %all-gather.12.cloned.1.call-start = ((), (), s32[]{:S(2)}) async-start(), calls=%async_computation.10 | async-start | bytes 7077888 | tf_op jit(solution)/shard_map/all_gather | solution.py:176
  53.3 200.3 %all-gather.10.cloned.1.call-start = ((), (), s32[]{:S(2)}) async-start(), calls=%async_computation.9 | async-start | bytes 7077888 | tf_op jit(solution)/shard_map/all_gather | solution.py:175
  53.9 592.4 %reduce-scatter.14.cloned.1.call-start = ((), (), s32[]{:S(2)}) async-start(), calls=%async_computation.15 | async-start | bytes 2359296 | tf_op jit(solution)/shard_map/reduce_scatter | solution.py:259
  56.0 49.7 %collective-permute-start = (bf16[256,2048]{1,0:T(8,128)(2,1)}, bf16[256,2048]{1,0:T(8,128)(2,1)}, u32[]{:S(2)}, u32[]{:S(2)}) collective-permute-start(bf16[256,2048]{1,0:T(8,128)(2,1)} %fusion.62), channel_id=1, source_target_pairs={{0,1},{1,0},{2,3},{3,2},{4,5},{5,4},{6,7},{7,6},{8,9},{9,8},{10,11... | collective-permute-start | bytes 3145736 | tf_op jit(solution)/shard_map/ppermute | solution.py:133
  56.9 48.8 %collective-permute-start.9 = (bf16[256,2048]{1,0:T(8,128)(2,1)S(1)}, bf16[256,2048]{1,0:T(8,128)(2,1)}, u32[]{:S(2)}, u32[]{:S(2)}) collective-permute-start(bf16[256,2048]{1,0:T(8,128)(2,1)S(1)} %copy-done.56), channel_id=1, source_target_pairs={{0,1},{1,2},{2,3},{3,0},{4,5},{5,6},{6,7},{7,4},{8,9},{9,10},{10,1... | collective-permute-start | bytes 3145736 | tf_op jit(solution)/shard_map/ppermute | solution.py:130
  105.7 68.4 %collective-permute-start.11 = (bf16[256,2048]{1,0:T(8,128)(2,1)}, bf16[256,2048]{1,0:T(8,128)(2,1)}, u32[]{:S(2)}, u32[]{:S(2)}) collective-permute-start(bf16[256,2048]{1,0:T(8,128)(2,1)} %collective-permute-done.9), channel_id=1, source_target_pairs={{0,1},{1,2},{2,3},{3,0},{4,5},{5,6},{6,7},{7,4},{8,9},{9,10},{10,1... | collective-permute-start | bytes 3145736 | tf_op jit(solution)/shard_map/ppermute | solution.py:130
  174.1 190.9 %collective-permute-start.13 = (bf16[256,2048]{1,0:T(8,128)(2,1)}, bf16[256,2048]{1,0:T(8,128)(2,1)}, u32[]{:S(2)}, u32[]{:S(2)}) collective-permute-start(bf16[256,2048]{1,0:T(8,128)(2,1)} %collective-permute-done.11), channel_id=1, source_target_pairs={{0,1},{1,2},{2,3},{3,0},{4,5},{5,6},{6,7},{7,4},{8,9},{9,10},{10,1... | collective-permute-start | bytes 3145736 | tf_op jit(solution)/shard_map/ppermute | solution.py:130
  200.5 62.0 %collective-permute-start.3 = (bf16[256,2048]{1,0:T(8,128)(2,1)S(1)}, bf16[256,2048]{1,0:T(8,128)(2,1)}, u32[]{:S(2)}, u32[]{:S(2)}) collective-permute-start(bf16[256,2048]{1,0:T(8,128)(2,1)S(1)} %multiply_convert_fusion), channel_id=1, source_target_pairs={{0,1},{1,2},{2,3},{3,0},{4,5},{5,6},{6,7},{7,4},{8,9},{9,10},{10,1... | collective-permute-start | bytes 3145736 | tf_op jit(solution)/shard_map/ppermute | solution.py:130
  285.1 50.6 %collective-permute-start.4 = (bf16[256,2048]{1,0:T(8,128)(2,1)S(1)}, bf16[256,2048]{1,0:T(8,128)(2,1)S(1)}, u32[]{:S(2)}, u32[]{:S(2)}) collective-permute-start(bf16[256,2048]{1,0:T(8,128)(2,1)S(1)} %convolution_convert_fusion.7), channel_id=1, source_target_pairs={{0,1},{1,2},{2,3},{3,0},{4,5},{5,6},{6,7},{7,4},{8,9},{9,10},{10,1... | collective-permute-start | bytes 3145736 | tf_op jit(solution)/shard_map/ppermute | solution.py:130
  290.8 67.4 %collective-permute-start.7 = (bf16[256,2048]{1,0:T(8,128)(2,1)S(1)}, bf16[256,2048]{1,0:T(8,128)(2,1)S(1)}, u32[]{:S(2)}, u32[]{:S(2)}) collective-permute-start(bf16[256,2048]{1,0:T(8,128)(2,1)S(1)} %collective-permute-done.5), channel_id=1, source_target_pairs={{0,1},{1,2},{2,3},{3,0},{4,5},{5,6},{6,7},{7,4},{8,9},{9,10},{10,1... | collective-permute-start | bytes 3145736 | tf_op jit(solution)/shard_map/ppermute | solution.py:130
  315.1 65.6 %collective-permute-start.12 = (bf16[256,2048]{1,0:T(8,128)(2,1)S(1)}, bf16[256,2048]{1,0:T(8,128)(2,1)S(1)}, u32[]{:S(2)}, u32[]{:S(2)}) collective-permute-start(bf16[256,2048]{1,0:T(8,128)(2,1)S(1)} %add_convert_fusion.1), channel_id=1, source_target_pairs={{0,1},{1,2},{2,3},{3,0},{4,5},{5,6},{6,7},{7,4},{8,9},{9,10},{10,1... | collective-permute-start | bytes 3145736 | tf_op jit(solution)/shard_map/ppermute | solution.py:130
  337.5 65.6 %collective-permute-start.6 = (bf16[256,2048]{1,0:T(8,128)(2,1)S(1)}, bf16[256,2048]{1,0:T(8,128)(2,1)S(1)}, u32[]{:S(2)}, u32[]{:S(2)}) collective-permute-start(bf16[256,2048]{1,0:T(8,128)(2,1)S(1)} %add_convert_fusion.4), channel_id=1, source_target_pairs={{0,1},{1,2},{2,3},{3,0},{4,5},{5,6},{6,7},{7,4},{8,9},{9,10},{10,1... | collective-permute-start | bytes 3145736 | tf_op jit(solution)/shard_map/ppermute | solution.py:130
  381.0 44.6 %collective-permute-start.14 = (bf16[256,2048]{1,0:T(8,128)(2,1)S(1)}, bf16[256,2048]{1,0:T(8,128)(2,1)S(1)}, u32[]{:S(2)}, u32[]{:S(2)}) collective-permute-start(bf16[256,2048]{1,0:T(8,128)(2,1)S(1)} %add_convert_fusion), channel_id=1, source_target_pairs={{0,1},{1,2},{2,3},{3,0},{4,5},{5,6},{6,7},{7,4},{8,9},{9,10},{10,1... | collective-permute-start | bytes 3145736 | tf_op jit(solution)/shard_map/ppermute | solution.py:130
  403.4 43.9 %collective-permute-start.8 = (bf16[256,2048]{1,0:T(8,128)(2,1)S(1)}, bf16[256,2048]{1,0:T(8,128)(2,1)S(1)}, u32[]{:S(2)}, u32[]{:S(2)}) collective-permute-start(bf16[256,2048]{1,0:T(8,128)(2,1)S(1)} %add_convert_fusion.3), channel_id=1, source_target_pairs={{0,1},{1,2},{2,3},{3,0},{4,5},{5,6},{6,7},{7,4},{8,9},{9,10},{10,1... | collective-permute-start | bytes 3145736 | tf_op jit(solution)/shard_map/ppermute | solution.py:130
  507.6 139.4 %reduce-scatter.10.cloned.1.call-start = ((), (), s32[]{:S(2)}) async-start(), calls=%async_computation.13 | async-start | bytes 4718592 | tf_op jit(solution)/shard_map/reduce_scatter | solution.py:259
  540.2 110.1 %reduce-scatter.12.cloned.1.call-start = ((), (), s32[]{:S(2)}) async-start(), calls=%async_computation.14 | async-start | bytes 2359296 | tf_op jit(solution)/shard_map/reduce_scatter | solution.py:259
  545.6 155.3 %reduce-scatter.8.cloned.1.call-start = ((), (), s32[]{:S(2)}) async-start(), calls=%async_computation.12 | async-start | bytes 4718592 | tf_op jit(solution)/shard_map/reduce_scatter | solution.py:259
  556.2 209.8 %reduce-scatter.16.cloned.1.call-start = ((), (), s32[]{:S(2)}) async-start(), calls=%async_computation.16 | async-start | bytes 7077888 | tf_op jit(solution)/shard_map/reduce_scatter | solution.py:259
  570.2 261.0 %reduce-scatter.18.cloned.1.call-start = ((), (), s32[]{:S(2)}) async-start(), calls=%async_computation.17 | async-start | bytes 7077888 | tf_op jit(solution)/shard_map/reduce_scatter | solution.py:259
  584.0 312.0 %reduce-scatter.20.cloned.1.call-start = ((), (), s32[]{:S(2)}) async-start(), calls=%async_computation.18 | async-start | bytes 7077888 | tf_op jit(solution)/shard_map/reduce_scatter | solution.py:259
  646.9 54.1 %collective-permute-start.22 = (bf16[256,1024]{1,0:T(8,128)(2,1)}, bf16[256,1024]{1,0:T(8,128)(2,1)S(1)}, u32[]{:S(2)}, u32[]{:S(2)}) collective-permute-start(bf16[256,1024]{1,0:T(8,128)(2,1)} %reduce-scatter.10.cloned.1.call-done), channel_id=1, source_target_pairs={{0,2},{1,3},{2,0},{3,1},{4,6},{5,7},{6,4},{7,5},{8,10},{9,11},{10,... | collective-permute-start | bytes 1572872 | tf_op jit(solution)/shard_map/ppermute | solution.py:311
  (136 other events, 1309.6 us)
Sparse Core Ops, SparseCore 0:
  12.4 49.2 all-gather.5
  64.1 46.5 all-gather.7
  112.7 46.5 all-gather.13
  161.0 45.4 all-gather.11
  208.2 45.3 all-gather.9
  507.7 39.2 reduce-scatter.13
  550.4 51.1 reduce-scatter.9
  604.9 41.5 reduce-scatter.11
  649.8 51.1 reduce-scatter.7
  704.2 61.7 reduce-scatter.15
  769.4 61.7 reduce-scatter.17
  834.4 61.5 reduce-scatter.19

commit v2 on v1

v2 whole, which is shorter than its diff:
```python
import functools
import math

import jax
import jax.numpy as jnp
from jax import lax
from jax.experimental import pallas as pl
from jax.experimental.pallas import tpu as pltpu
from jax.sharding import PartitionSpec as P

EPSILON = 1e-06
THETA = 1000000.0
MASKED = -1e30


def rms_scale(value_rows, norm_gain):
    return (
        value_rows
        * lax.rsqrt(jnp.mean(value_rows * value_rows, axis=-1, keepdims=True) + EPSILON)
        * norm_gain
    )


def doc_starts(segments):
    length = segments.shape[-1]
    indices = jnp.arange(length, dtype=jnp.int32)
    leading = jnp.ones(segments.shape[:-1] + (1,), dtype=jnp.bool_)
    change = jnp.concatenate([leading, segments[..., 1:] != segments[..., :-1]], axis=-1)
    return lax.cummax(jnp.where(change, indices, jnp.int32(0)), axis=segments.ndim - 1)


def contract(left_side, right_side, left_dim, right_dim):
    return lax.dot_general(
        left_side,
        right_side,
        (((left_dim,), (right_dim,)), ((), ())),
        preferred_element_type=jnp.float32,
    )


def inverse_rms(rows):
    return lax.rsqrt(jnp.mean(rows * rows, axis=-1, keepdims=True) + EPSILON)


def head_columns(head, size):
    return slice(head * size, (head + 1) * size)


def mix_specs(full, rows, group, heads, size):
    width = full.shape[0]
    return [
        pl.BlockSpec((width, (group + 2) * size), lambda h: (0, h)),
        pl.BlockSpec((width, group * size), lambda h: (0, heads * (group + 2) // group + h)),
    ]


def table_specs(rows, size):
    return [
        pl.BlockSpec((rows, size), lambda h: (0, 0)),
        pl.BlockSpec((rows, size), lambda h: (0, 0)),
        pl.BlockSpec((1, size), lambda h: (0, 0)),
        pl.BlockSpec((1, size), lambda h: (0, 0)),
        pl.BlockSpec((rows, 1), lambda h: (0, 0)),
        pl.BlockSpec((rows, 1), lambda h: (0, 0)),
        pl.BlockSpec((1, rows), lambda h: (0, 0)),
    ]


def weights_of(query, key, allowed, size):
    scores = contract(query, key, 1, 1) * (1.0 / math.sqrt(size))
    exponent = jnp.exp(jnp.where(allowed, scores, MASKED))
    return exponent * (1.0 / jnp.sum(exponent, axis=-1, keepdims=True))


def once(shape):
    return pl.BlockSpec(shape, lambda h: (0, 0), pipeline_mode=pl.Buffered(1))


def sum_shapes(rows, width, own_rows, last):
    if not last:
        return [jax.ShapeDtypeStruct((rows, width), jnp.float32)]
    return [
        jax.ShapeDtypeStruct((own_rows, width), jnp.float32),
        jax.ShapeDtypeStruct((rows - own_rows, width), jnp.bfloat16),
    ]


def put_sum(head, heads, term, before_refs, total_ref, out_refs):
    @pl.when(head == 0)
    def _():
        total_ref[...] = term + before_refs[0][...] if before_refs else term

    @pl.when(head > 0)
    def _():
        total_ref[...] += term

    if len(out_refs) == 2:

        @pl.when(head == heads - 1)
        def _():
            own_rows = out_refs[0].shape[0]
            out_refs[0][...] = total_ref[:own_rows]
            out_refs[1][...] = total_ref[own_rows:].astype(jnp.bfloat16)


def mixer_forward(rows_in, full, tables, group, heads, before, own_rows, last):
    rows, width = rows_in.shape
    size = tables[0].shape[1]
    low = jnp.bfloat16
    wide, thin, kept = (group + 2) * size, group * size, (group + 1) * size

    def kernel(x_ref, w_ref, o_ref, cos_ref, sin_ref, qg_ref, kg_ref, tok_ref, lo_ref, col_ref,
               *refs):
        before_refs, refs = refs[: len(before)], refs[len(before) :]
        raw_ref, rot_ref, att_ref = refs[:3]
        sum_refs, total_ref = (refs[3:5], refs[5]) if last else (refs[3:4], refs[3])
        head = pl.program_id(0)
        raw = jnp.dot(x_ref[...], w_ref[...], preferred_element_type=jnp.float32)
        raw_ref[...] = raw[:, :kept]
        value = raw[:, kept:].astype(low)
        cosine, sine = cos_ref[...], sin_ref[...]
        turned = []
        for part in range(group + 1):
            vector = raw[:, head_columns(part, size)]
            gain = qg_ref[...] if part < group else kg_ref[...]
            vector = vector * inverse_rms(vector) * gain
            turned.append(
                (vector * cosine + pltpu.roll(vector, size // 2, 1) * sine).astype(low)
            )
        for part in range(group + 1):
            rot_ref[:, head_columns(part, size)] = turned[part]
        rot_ref[:, head_columns(group + 1, size)] = value
        allowed = (tok_ref[...] >= col_ref[...]) & (lo_ref[...] <= col_ref[...])
        for part in range(group):
            share = weights_of(turned[part], turned[group], allowed, size).astype(low)
            att_ref[:, head_columns(part, size)] = jnp.dot(
                share, value, preferred_element_type=jnp.float32
            ).astype(low)
        term = contract(att_ref[...], o_ref[...], 1, 1)
        put_sum(head, heads, term, before_refs, total_ref, sum_refs)

    sums = sum_shapes(rows, width, own_rows, last)

    return pl.pallas_call(
        kernel,
        out_shape=(
            jax.ShapeDtypeStruct((rows, heads * kept), jnp.float32),
            jax.ShapeDtypeStruct((rows, heads * wide), low),
            jax.ShapeDtypeStruct((rows, heads * thin), low),
            *sums,
        ),
        grid=(heads,),
        in_specs=[once((rows, width))]
        + mix_specs(full, rows, group, heads, size)
        + table_specs(rows, size)
        + [once((rows, width)) for _ in before],
        out_specs=(
            pl.BlockSpec((rows, kept), lambda h: (0, h)),
            pl.BlockSpec((rows, wide), lambda h: (0, h)),
            pl.BlockSpec((rows, thin), lambda h: (0, h)),
            *[once(item.shape) for item in sums],
        ),
        scratch_shapes=[pltpu.VMEM((rows, width), jnp.float32)] if last else [],
        cost_estimate=pl.CostEstimate(
            flops=2 * rows * heads * (width * (wide + thin) + 2 * rows * thin),
            bytes_accessed=2 * width * heads * (wide + thin) + 8 * rows * width,
            transcendentals=rows * rows * heads * group,
        ),
        name="mixer_forward",
    )(rows_in, full, full, *tables, *before)


def mixer_backward(
    back_rows, full, tables, raw, rotated, attended, group, heads, before, source, own_rows
):
    last = bool(source)
    rows, width = back_rows.shape
    size = tables[0].shape[1]
    low = jnp.bfloat16
    wide, thin, kept = (group + 2) * size, group * size, (group + 1) * size
    scale = 1.0 / math.sqrt(size)

    def kernel(g_ref, w_ref, o_ref, cos_ref, sin_ref, qg_ref, kg_ref, tok_ref, lo_ref, col_ref,
               raw_ref, rot_ref, att_ref, *refs):
        before_refs, refs = refs[: len(before)], refs[len(before) :]
        source_refs, refs = refs[: len(source)], refs[len(source) :]
        low_ref, gain_ref = refs[:2]
        sum_refs, total_ref = (refs[2:4], refs[5]) if last else (refs[2:3], refs[2])
        head = pl.program_id(0)

        @pl.when(head == 0)
        def _():
            gain_ref[...] = jnp.zeros_like(gain_ref)

        attended_back = jnp.dot(
            g_ref[...], o_ref[...], preferred_element_type=jnp.float32
        ).astype(low)
        key = rot_ref[:, head_columns(group, size)]
        value = rot_ref[:, head_columns(group + 1, size)]
        cosine, sine = cos_ref[...], sin_ref[...]
        allowed = (tok_ref[...] >= col_ref[...]) & (lo_ref[...] <= col_ref[...])

        def unturn(part, turned_back, gain, row):
            vector = raw_ref[:, head_columns(part, size)]
            back = turned_back * cosine + pltpu.roll(turned_back * sine, size // 2, 1)
            inverse = inverse_rms(vector)
            gain_ref[row : row + 1, :] += jnp.sum(
                back * vector * inverse, axis=0, keepdims=True
            )
            back = back * gain
            shift = jnp.mean(back * vector, axis=-1, keepdims=True) * inverse * inverse
            low_ref[:, head_columns(part, size)] = ((back - vector * shift) * inverse).astype(low)

        key_back = jnp.zeros((rows, size), jnp.float32)
        value_back = jnp.zeros((rows, size), jnp.float32)
        for part in range(group):
            query = rot_ref[:, head_columns(part, size)]
            back = attended_back[:, head_columns(part, size)]
            delta = jnp.sum(
                back.astype(jnp.float32)
                * att_ref[:, head_columns(part, size)].astype(jnp.float32),
                axis=-1,
                keepdims=True,
            )
            share = weights_of(query, key, allowed, size)
            score_back = (share * (contract(back, value, 1, 1) - delta)).astype(low)
            value_back += contract(share.astype(low), back, 0, 0)
            key_back += contract(score_back, query, 0, 0)
            query_back = jnp.dot(score_back, key, preferred_element_type=jnp.float32) * scale
            unturn(part, query_back, qg_ref[...], 0)
        unturn(group, key_back * scale, kg_ref[...], 1)
        low_ref[:, head_columns(group + 1, size)] = value_back.astype(low)
        term = contract(low_ref[...], w_ref[...], 1, 1)
        put_sum(head, heads, term, before_refs, total_ref, sum_refs)
        if last:

            @pl.when(head == heads - 1)
            def _():
                rows_float = source_refs[0][...].astype(jnp.float32)
                unit = rows_float * inverse_rms(rows_float)
                refs[4][...] = jnp.sum(total_ref[...] * unit, axis=0, keepdims=True)

    sums = sum_shapes(rows, width, own_rows, last)
    if last:
        sums.append(jax.ShapeDtypeStruct((1, width), jnp.float32))

    return pl.pallas_call(
        kernel,
        out_shape=(
            jax.ShapeDtypeStruct((rows, heads * wide), low),
            jax.ShapeDtypeStruct((8, size), jnp.float32),
            *sums,
        ),
        grid=(heads,),
        in_specs=[once((rows, width))]
        + mix_specs(full, rows, group, heads, size)
        + table_specs(rows, size)
        + [
            pl.BlockSpec((rows, kept), lambda h: (0, h)),
            pl.BlockSpec((rows, wide), lambda h: (0, h)),
            pl.BlockSpec((rows, thin), lambda h: (0, h)),
        ]
        + [once((rows, width)) for _ in before + source],
        out_specs=(
            pl.BlockSpec((rows, wide), lambda h: (0, h)),
            pl.BlockSpec((8, size), lambda h: (0, 0)),
            *[once(item.shape) for item in sums],
        ),
        scratch_shapes=[pltpu.VMEM((rows, width), jnp.float32)] if last else [],
        cost_estimate=pl.CostEstimate(
            flops=2 * rows * heads * (width * (wide + thin) + 5 * rows * thin),
            bytes_accessed=2 * width * heads * (wide + thin) + 8 * rows * width,
            transcendentals=rows * rows * heads * group,
        ),
        name="mixer_backward",
    )(back_rows, full, full, *tables, raw, rotated, attended, *before, *source)


def block_product(block_ids, block, lefts, rights, received, split):
    low = jnp.bfloat16
    count = block_ids.shape[0]
    out_width = sum(group[0].shape[1] for group in rights)
    flat = [piece for group in rights for piece in group]
    tokens = sum(piece.shape[0] for piece in lefts)
    rest = count - split

    def kernel(ids_ref, *refs):
        left_refs, refs = refs[: len(lefts)], refs[len(lefts) :]
        right_refs, refs = refs[: len(flat)], refs[len(flat) :]
        columns, taken = [], 0
        for group in rights:
            pieces = [ref[...] for ref in right_refs[taken : taken + len(group)]]
            columns.append(jnp.concatenate(pieces, axis=0) if len(pieces) > 1 else pieces[0])
            taken += len(group)
        left = [ref[...] for ref in left_refs]
        left = jnp.concatenate(left, axis=0) if len(left) > 1 else left[0]
        outs = refs[1:] if received is not None else refs
        at = 0
        for column in columns:
            span = slice(at, at + column.shape[1])
            at = span.stop
            total = contract(left, column, 0, 0)
            if received is not None:
                total = total + refs[0][:, span].astype(jnp.float32)
            if rest == 0:
                outs[0][:, span] = total.astype(low)
                continue

            @pl.when(pl.program_id(0) < split)
            def _(total=total, span=span):
                outs[0][:, span] = total.astype(low)

            @pl.when(pl.program_id(0) >= split)
            def _(total=total, span=span):
                outs[1][:, span] = total

    out_shape = [jax.ShapeDtypeStruct((split * block, out_width), low)]
    out_specs = [
        pl.BlockSpec((block, out_width), lambda i, ids: (jnp.minimum(i, split - 1), 0))
    ]
    if rest:
        out_shape.append(jax.ShapeDtypeStruct((rest * block, out_width), jnp.float32))
        out_specs.append(
            pl.BlockSpec((block, out_width), lambda i, ids: (jnp.maximum(i - split, 0), 0))
        )
    extra = [] if received is None else [received]
    return pl.pallas_call(
        kernel,
        out_shape=out_shape,
        grid_spec=pltpu.PrefetchScalarGridSpec(
            num_scalar_prefetch=1,
            grid=(count,),
            in_specs=[
                pl.BlockSpec((piece.shape[0], block), lambda i, ids: (0, ids[i]))
                for piece in lefts
            ]
            + [pl.BlockSpec(piece.shape, lambda i, ids: (0, 0)) for piece in flat]
            + [pl.BlockSpec((block, out_width), lambda i, ids: (i, 0)) for _ in extra],
            out_specs=out_specs,
        ),
        cost_estimate=pl.CostEstimate(
            flops=2 * tokens * count * block * out_width,
            bytes_accessed=2 * tokens * (count * block + out_width)
            + 4 * count * block * out_width,
            transcendentals=0,
        ),
        name="block_product",
    )(block_ids, *lefts, *flat, *extra)


def after(value, *others):
    return lax.optimization_barrier((value,) + others)[0]


class Chain:
    def __init__(self):
        self.last = None

    def gate(self, value):
        return value if self.last is None else after(value, self.last)

    def mark(self, value):
        self.last = value
        return value


def halving_masks(bits):
    if not bits:
        return [0]
    rest = halving_masks(bits[1:])
    return [bits[0] ^ mask for mask in rest] + rest


def block_orders(fsdp):
    bits = [1 << k for k in range(1, fsdp.bit_length() - 1)]
    orders = (bits, bits[::-1])
    chip = lax.axis_index("fsdp")
    even, odd = (jnp.array(halving_masks(b), jnp.int32) for b in orders)
    own = chip % 2 == 0
    return orders, chip ^ 1 ^ jnp.where(own, odd, even), chip ^ jnp.where(own, even, odd)


class Doubling:
    def __init__(self, fsdp, piece):
        self.size, self.piece = fsdp, piece
        self.orders, self.far_ids, self.near_ids = block_orders(fsdp)
        self.left = len(self.orders[0])
        self.start()

    def start(self):
        self.left -= 1
        if self.left >= 0:
            pairs = [(r, r ^ self.orders[r % 2][self.left]) for r in range(self.size)]
        else:
            pairs = [(r, r ^ 1) for r in range(self.size)]
        self.moved = lax.ppermute(self.piece, "fsdp", pairs)

    def next(self, token):
        self.piece = jnp.concatenate([after(self.moved, token), self.piece], axis=0)
        self.start()

    def whole(self, token):
        half, columns = self.piece.shape
        count = self.size // 2
        block = half // count

        def kernel(ids_ref, far_ref, near_ref, out_ref):
            @pl.when(pl.program_id(0) < count)
            def _():
                out_ref[...] = far_ref[...]

            @pl.when(pl.program_id(0) >= count)
            def _():
                out_ref[...] = near_ref[...]

        return pl.pallas_call(
            kernel,
            out_shape=jax.ShapeDtypeStruct((2 * half, columns), self.piece.dtype),
            grid_spec=pltpu.PrefetchScalarGridSpec(
                num_scalar_prefetch=1,
                grid=(2 * count,),
                in_specs=[
                    pl.BlockSpec((block, columns), lambda i, ids: (jnp.minimum(i, count - 1), 0)),
                    pl.BlockSpec((block, columns), lambda i, ids: (jnp.maximum(i - count, 0), 0)),
                ],
                out_specs=pl.BlockSpec((block, columns), lambda i, ids: (ids[i], 0)),
            ),
            cost_estimate=pl.CostEstimate(
                flops=0, bytes_accessed=8 * half * columns, transcendentals=0
            ),
            name="placed",
        )(jnp.concatenate([self.far_ids, self.near_ids]), after(self.moved, token), self.piece)


class Halving:
    def __init__(self, chain, fsdp, lefts, rights):
        self.chain, self.size = chain, fsdp
        self.lefts, self.rights = lefts, rights
        self.block = lefts[0].shape[1] // fsdp
        self.orders, self.sent_ids, self.kept_ids = block_orders(fsdp)
        self.step = 0

    def send(self):
        lefts = [self.chain.gate(self.lefts[0])] + self.lefts[1:]
        (sent,) = block_product(
            self.sent_ids, self.block, lefts, self.rights, None, self.size // 2
        )
        self.chain.mark(sent)
        self.moved = lax.ppermute(sent, "fsdp", [(r, r ^ 1) for r in range(self.size)])

    def keep(self):
        moved = self.chain.gate(self.moved)
        sent, self.rest = block_product(
            self.kept_ids, self.block, self.lefts, self.rights, moved, self.size // 4
        )
        self.chain.mark(sent)
        self.exchange(sent)

    def exchange(self, sent):
        self.moved = lax.ppermute(
            sent,
            "fsdp",
            [(r, r ^ self.orders[r % 2][self.step]) for r in range(self.size)],
        )
        self.step += 1

    def add(self):
        total = self.rest + self.chain.gate(self.moved).astype(jnp.float32)
        if self.step == len(self.orders[0]):
            self.chain.mark(total)
            return total
        half = total.shape[0] // 2
        sent, self.rest = total[:half].astype(jnp.bfloat16), total[half:]
        self.chain.mark(sent)
        self.exchange(sent)
        return None

    def finish(self):
        total = None
        while total is None:
            total = self.add()
        return total


def shards(
    sizes,
    layer_input,
    segments,
    cotangent,
    attention_gain,
    query_weight,
    key_matrix,
    value_matrix,
    query_norm_gain,
    key_gain,
    output_matrix,
    hidden_gain,
    gate_weight,
    up_weight,
    down_weight,
):
    fsdp, tp = sizes
    low = jnp.bfloat16
    own_rows, width = layer_input.shape
    seq_count, seq_length = segments.shape
    size = query_norm_gain.shape[0]
    team = tp // seq_count
    sets = seq_count
    me = lax.axis_index("tp")
    place = me % team
    chain = Chain()

    def hop(value):
        return lax.ppermute(value, "tp", [(i, (i + 1) % tp) for i in range(tp)])

    def team_hop(value, step):
        return lax.ppermute(
            value, "tp", [(i, i // team * team + (i + step) % team) for i in range(tp)]
        )

    def team_rows(own):
        return jnp.concatenate([own] + [team_hop(own, step) for step in range(1, team)], axis=0)

    def team_send(others):
        return [
            team_hop(others[k * own_rows : (k + 1) * own_rows], team - 1 - k)
            for k in range(team - 1)
        ]

    def total_of(own, moved):
        for part in moved:
            own = own + part.astype(jnp.float32)
        return own

    def ring_rows(own, tokens):
        blocks = [own]
        for _, token in zip(range(1, tp), tokens):
            blocks.append(hop(blocks[-1] if token is None else after(blocks[-1], token)))
        return blocks

    query_width = query_weight.shape[1]
    key_width = key_matrix.shape[1]
    mix_width = query_width + 2 * key_width
    heads = key_width // size
    group = query_width // key_width
    thin = group * size

    source = team_rows(layer_input)
    columns = []
    for head in range(heads):
        columns += [
            query_weight[:, head_columns(head, thin)],
            key_matrix[:, head_columns(head, size)],
            value_matrix[:, head_columns(head, size)],
        ]
    own_set = jnp.concatenate(columns + [output_matrix.T], axis=1)
    weight_sets = [own_set] + [
        lax.ppermute(
            own_set,
            "tp",
            [(i, (i // team + m) % sets * team + i % team) for i in range(tp)],
        )
        for m in range(1, sets)
    ]
    weight_sets[1:] = [after(w, source) for w in weight_sets[1:]]
    set_full = [lax.all_gather(w, "fsdp", axis=0, tiled=True) for w in weight_sets]
    down_full = lax.all_gather(after(down_weight, *weight_sets), "fsdp", axis=1, tiled=True)
    gate_gather = Doubling(fsdp, gate_weight)
    up_gather = Doubling(fsdp, up_weight)

    source_float = source.astype(jnp.float32)
    input_float = layer_input.astype(jnp.float32)
    attention_rows = rms_scale(source_float, attention_gain).astype(low)

    own_starts = doc_starts(lax.dynamic_index_in_dim(segments, me // team, 0, keepdims=False))
    firsts = [(place + team - step) % team * own_rows for step in range(team)]
    tokens = jnp.concatenate([first + jnp.arange(own_rows, dtype=jnp.int32) for first in firsts])
    starts = jnp.concatenate(
        [lax.dynamic_slice_in_dim(own_starts, first, own_rows) for first in firsts]
    )
    exponents = jnp.arange(size // 2, dtype=jnp.float32) * (-2.0 / size)
    frequencies = jnp.power(jnp.float32(THETA), exponents)
    angles = (tokens - starts).astype(jnp.float32)[:, None] * frequencies
    cosine, sine = jnp.cos(angles), jnp.sin(angles)
    tables = (
        jnp.concatenate([cosine, cosine], axis=1),
        jnp.concatenate([-sine, sine], axis=1),
        query_norm_gain[None],
        key_gain[None],
        tokens[:, None],
        starts[:, None],
        tokens[None],
    )

    for gather in (gate_gather, up_gather):
        gather.next(attention_rows)
    saved, mixed = [], []
    for m, full in enumerate(set_full):
        raw, rotated, attended, *mixed = mixer_forward(
            chain.gate(attention_rows), full, tables, group, heads, mixed, own_rows, m == sets - 1
        )
        chain.mark(attended)
        saved.append((raw, rotated, attended))
        if m == 0:
            for gather in (gate_gather, up_gather):
                while gather.left >= 0:
                    gather.next(attended)
    moved_mixed = team_send(mixed[1])
    gate_full, up_full = (gather.whole(mixed[1]) for gather in (gate_gather, up_gather))
    mid = input_float + total_of(mixed[0], moved_mixed)
    hidden_in = rms_scale(mid, hidden_gain).astype(low)

    cotangent_blocks = ring_rows(
        cotangent, [weight_sets[-1], saved[0][2]] + [saved[-1][2]] * (tp - 3)
    )
    hidden_blocks = ring_rows(after(hidden_in, cotangent_blocks[-1]), [None] * tp)
    in_parts, hiddens, gate_backs, up_backs = [], [], [], []
    for cotangent_rows, hidden_rows in zip(cotangent_blocks, hidden_blocks):
        hidden_rows = chain.gate(hidden_rows)
        gate_value = jnp.dot(hidden_rows, gate_full, preferred_element_type=jnp.float32)
        up_value = jnp.dot(hidden_rows, up_full, preferred_element_type=jnp.float32)
        hidden_back = contract(cotangent_rows, down_full, 1, 1)
        sigmoid = jax.nn.sigmoid(gate_value)
        hidden = (gate_value * sigmoid * up_value).astype(low)
        gate_back = (
            hidden_back * up_value * sigmoid * (1.0 + gate_value * (1.0 - sigmoid))
        ).astype(low)
        up_back = (hidden_back * gate_value * sigmoid).astype(low)
        hiddens.append(hidden)
        gate_backs.append(gate_back)
        up_backs.append(up_back)
        in_parts.append(
            chain.mark(contract(gate_back, gate_full, 1, 1) + contract(up_back, up_full, 1, 1))
        )

    down_grad = Halving(chain, fsdp, cotangent_blocks, [hiddens])
    gate_grad = Halving(chain, fsdp, hidden_blocks, [gate_backs])
    up_grad = Halving(chain, fsdp, hidden_blocks, [up_backs])
    fillers = [down_grad.send, gate_grad.send, down_grad.keep, up_grad.send]
    carried = in_parts[1]
    for step in range(2, tp + 1):
        arrived = hop(carried.astype(low))
        if step > 2:
            for fill in fillers[:2]:
                fill()
            fillers = fillers[2:]
        carried = chain.mark(chain.gate(arrived).astype(jnp.float32) + in_parts[step % tp])
    hidden_in_back = carried

    mid_part, hidden_gain_part = jax.vjp(rms_scale, mid, hidden_gain)[1](hidden_in_back)
    mid_back = cotangent.astype(jnp.float32) + mid_part
    mixer_own = chain.mark(mid_back.astype(low))
    mixer_rows = team_rows(mixer_own)
    for fill in fillers + [gate_grad.keep, up_grad.keep]:
        fill()

    out_parts = [
        jnp.dot(hidden, down_full, preferred_element_type=jnp.float32) for hidden in hiddens
    ]
    out_moved = [hop(after(out_parts[1].astype(low), mixer_rows))]

    def out_step():
        step = len(out_moved) + 1
        total = chain.gate(out_moved[-1]).astype(jnp.float32) + out_parts[step % tp]
        if step < tp:
            out_moved.append(hop(chain.mark(total.astype(low))))
        return total

    in_back, gain_parts = [], None
    mix_grads = [None] * sets
    for m in list(range(1, sets)) + [0]:
        raw, rotated, attended = saved[m]
        mix_low, gain_add, *in_back = mixer_backward(
            chain.gate(mixer_rows),
            set_full[m],
            tables,
            raw,
            rotated,
            attended,
            group,
            heads,
            in_back,
            [source] if m == 0 else [],
            own_rows,
        )
        chain.mark(mix_low)
        gain_parts = gain_add if gain_parts is None else gain_parts + gain_add
        mix_grads[m] = Halving(chain, fsdp, [attention_rows], [[mix_low]])
        if m > 0:
            mix_grads[m].send()
        if m == 1:
            down_grad.add()
            out_step()
    own_back, others_back, attention_gain_part = in_back
    moved_back = team_send(others_back)
    output_grad = Halving(chain, fsdp, [mixer_rows], [[kept[2]] for kept in saved])
    mix_grads[0].send()
    for m in range(1, sets):
        mix_grads[m].keep()
    output_grad.send()
    gate_grad.add()
    up_grad.add()
    mix_grads[0].keep()
    output_grad.keep()
    down_sum = down_grad.finish()
    while len(out_moved) < tp - 1:
        out_step()

    gains = jnp.concatenate(
        [attention_gain_part[0], hidden_gain_part, gain_parts[0], gain_parts[1]]
    )
    for axis, extent in (("fsdp", fsdp), ("tp", tp)):
        bit = 1
        while bit < extent:
            moved = lax.ppermute(gains, axis, [(i, i ^ bit) for i in range(extent)])
            gains = chain.mark(gains + chain.gate(moved))
            bit *= 2

    attention_in_back = total_of(own_back, [chain.gate(part) for part in moved_back])
    input_part = jax.vjp(lambda rows: rms_scale(rows, attention_gain), input_float)[1](
        attention_in_back
    )[0]
    input_gradient = chain.mark((mid_back + input_part).astype(low))

    for grad in mix_grads[1:] + [output_grad, mix_grads[0]]:
        if grad.step < len(grad.orders[0]):
            grad.add()
    gate_sum, up_sum = (grad.finish() for grad in (gate_grad, up_grad))
    mix_sums = [mix_grads[m].finish() for m in range(1, sets)]
    output_parts = output_grad.finish()
    mix_sums = [mix_grads[0].finish()] + mix_sums
    output_parts = [output_parts[:, head_columns(m, query_width)] for m in range(sets)]
    layer_output = (mid + out_step()).astype(low)

    total = jnp.concatenate([mix_sums[0], output_parts[0]], axis=1)
    for m in range(1, sets):
        moved = lax.ppermute(
            jnp.concatenate([mix_sums[m], output_parts[m]], axis=1).astype(low),
            "tp",
            [(i, (i // team + sets - m) % sets * team + i % team) for i in range(tp)],
        )
        total = total + moved.astype(jnp.float32)
    wide = thin + 2 * size
    query_sum, key_sum, value_sum = (
        jnp.concatenate(
            [total[:, head * wide + at : head * wide + at + span] for head in range(heads)],
            axis=1,
        )
        for at, span in ((0, thin), (thin, size), (thin + size, size))
    )
    output_sum = total[:, mix_width:].T

    return (
        layer_output,
        input_gradient,
        gains[:width],
        query_sum,
        key_sum,
        value_sum,
        gains[2 * width : 2 * width + size],
        gains[2 * width + size :],
        output_sum,
        gains[width : 2 * width],
        gate_sum,
        up_sum,
        down_sum.T,
    )


def solution(mesh):
    rows = P(("fsdp", "tp"), None)
    by_row, by_column = P("fsdp", "tp"), P("tp", "fsdp")
    in_specs = (
        (rows, P("fsdp", None), rows, P())
        + (by_row,) * 3
        + (P(), P(), by_column, P(), by_row, by_row, by_column)
    )
    out_specs = (
        (rows, rows, P())
        + (by_row,) * 3
        + (P(), P(), by_column, P(), by_row, by_row, by_column)
    )
    return jax.shard_map(
        functools.partial(shards, (mesh.shape["fsdp"], mesh.shape["tp"])),
        mesh=mesh,
        in_specs=in_specs,
        out_specs=out_specs,
        check_vma=False,
    )
```

time: 915 us -> 712 us (0.78)
  waiting for transfers between devices: 546 us -> 290 us
  Pallas kernels: 0 us -> 183 us
  matrix products: 203 us -> 81.4 us
  local copies, waits for them, and re-layouts: 62.8 us -> 31.8 us
  starting transfers between devices: 24.5 us -> 46.3 us
    reduce_scatter x7 -> x0, waiting for transfers between devices: 226 us -> none  [scatter(): lax.psum_scatter(value.astype(low), 'fsdp', scatter_dimension=dim, tiled=...]
    pallas_call x0 -> x18, Pallas kernels: none -> 183 us  [the longest x12 90.4 us: block_product(): pl.pallas_call(kernel, out_shape=out_shape, grid_spec=pltpu.PrefetchScala...]
    dot_general x23 -> x12, matrix products: 117 us -> 36.2 us  [contract(): lax.dot_general(left_side, right_side, (((left_dim,), (right_dim,)), ((),...]
    dot_general x14 -> x0, matrix products: 36.4 us -> none  [the longest x2 10.9 us: shards(): jnp.dot(attention_rows, full[:, :mix_width], preferred_element_type=jnp.f...]
    all_gather x3 -> x1, waiting for transfers between devices: 45.6 us -> 9.32 us  [shards(): lax.all_gather(after(down_weight, *weight_sets), 'fsdp', axis=1, tiled=True)]
    ppermute x1, waiting for transfers between devices: 34.6 us -> 0.01 us  [shards(): lax.ppermute(own_set, 'tp', [(i, (i // team + m) % sets * team + i % team...]
    ppermute x19 -> x42, waiting for transfers between devices: 175 us -> 210 us  [the longest x12 87.1 us: hop(): return lax.ppermute(value, 'tp', [(i, (i + 1) % tp) for i in range(tp)])]
    add x9 -> x22, other arithmetic: 1.25 us -> 21.2 us  [the longest x12 17.5 us: add(): total = self.rest + self.chain.gate(self.moved).astype(jnp.float32)]
  transfers between devices with their start and end apart: 36 -> 50, of which waited for: 25 -> 20; matrix products, arithmetic and copies ran while one was open for 29% -> 21% of each run, Pallas kernels for 0% -> 25%
where the time goes in v2:
time: 712 us; the launch traced here: 703 us
  waiting for transfers between devices  290 us (41%)
  Pallas kernels  183 us (26%)
  matrix products  81.4 us (11%)
  other arithmetic  55.9 us (8%)
  starting transfers between devices  46.3 us (7%)
  local copies, waits for them, and re-layouts  31.8 us (4%)
  between operations  15 us (2%)
    pallas_call x12, Pallas kernels, block_product(): pl.pallas_call(kernel, out_shape=out_shape, grid_spec=pltpu.PrefetchScala...  90.4 us
    ppermute x12, waiting for transfers between devices, hop(): return lax.ppermute(value, 'tp', [(i, (i + 1) % tp) for i in range(tp)])  87.1 us
    ppermute x4, waiting for transfers between devices, team_hop(): lax.ppermute(value, 'tp', [(i, i // team * team + (i + step) % team) for...  69.7 us
    ppermute x12, waiting for transfers between devices, exchange(): lax.ppermute(sent, 'fsdp', [(r, r ^ self.orders[r % 2][self.step]) for r...  43.6 us
    pallas_call x2, Pallas kernels, mixer_backward(): pl.pallas_call(kernel, out_shape=(jax.ShapeDtypeStruct((rows, heads * wid...  39.5 us
    dot_general x12, matrix products, contract(): lax.dot_general(left_side, right_side, (((left_dim,), (right_dim,)), ((),...  36.2 us
    pallas_call x2, Pallas kernels, mixer_forward(): pl.pallas_call(kernel, out_shape=(jax.ShapeDtypeStruct((rows, heads * kep...  34.9 us
    ppermute x6, waiting for transfers between devices, start(): self.moved = lax.ppermute(self.piece, 'fsdp', pairs)  33.7 us
  transfers between devices with their start and end apart: 50, of which 20 were waited for; matrix products, arithmetic and copies ran while one was open for 21% of the time, Pallas kernels for 25%

profile of v2, /device:TPU:0, one launch (start us, length us, event | category | flops | bytes accessed | tf_op | source)
XLA Modules:
  0.0 702.9 jit_solution(14403940197513925463)
XLA Ops:
  20.5 37.3 %collective-permute-done = bf16[256,2048]{1,0:T(8,128)(2,1)S(1)} collective-permute-done((bf16[256,2048]{1,0:T(8,128)(2,1)S(1)}, bf16[256,2048]{1,0:T(8,128)(2,1)S(1)}, u32[]{:S(2)}, u32[]{:S(2)}) %collective-permute-start) | collective-permute-done | bytes 1048608 | tf_op jit(solution)/shard_map/ppermute | solution.py:517
  77.7 14.6 %collective-permute-done.7 = bf16[256,1536]{1,0:T(8,128)(2,1)} collective-permute-done((bf16[256,1536]{1,0:T(8,128)(2,1)}, bf16[256,1536]{1,0:T(8,128)(2,1)}, u32[]{:S(2)}, u32[]{:S(2)}) %collective-permute-start.7) | collective-permute-done | bytes 786464 | tf_op jit(solution)/shard_map/ppermute | solution.py:396
  102.4 16.7 %mixer_forward.2 = (f32[512,768]{1,0:T(8,128)}, bf16[512,1024]{1,0:T(8,128)(2,1)}, bf16[512,512]{1,0:T(8,128)(2,1)}, f32[512,2048]{1,0:T(8,128)}) custom-call(bf16[512,2048]{1,0:T(8,128)(2,1)} %fusion.2.x_ref.refs_0_, bf16[2048,1536]{1,0:T(8,128)(2,1)} %all-gather.4.cloned.1.call-done.w_ref.o_ref, ...), custom_call_target="tpu_custom_call" | custom-call | flops 3758096384 | bytes 14680064 | tf_op jit(solution)/shard_map/mixer_forward/pallas_call | solution.py:144
  124.9 12.1 %collective-permute-done.8 = bf16[512,1536]{1,0:T(8,128)(2,1)} collective-permute-done((bf16[512,1536]{1,0:T(8,128)(2,1)}, bf16[512,1536]{1,0:T(8,128)(2,1)}, u32[]{:S(2)}, u32[]{:S(2)}) %collective-permute-start.8) | collective-permute-done | bytes 1572896 | tf_op jit(solution)/shard_map/ppermute | solution.py:396
  146.6 18.2 %mixer_forward.3 = (f32[512,768]{1,0:T(8,128)}, bf16[512,1024]{1,0:T(8,128)(2,1)}, bf16[512,512]{1,0:T(8,128)(2,1)}, f32[256,2048]{1,0:T(8,128)}, bf16[256,2048]{1,0:T(8,128)(2,1)}) custom-call(bf16[512,2048]{1,0:T(8,128)(2,1)} %fusion.2.x_ref.refs_0_, bf16[2048,1536]{1,0:T(8,128)(2,1)} %all-gather.6.cloned.1.call-done.w_ref.o_ref, ...), custom_call_target="tpu_custom_call" | custom-call | flops 3758096384 | bytes 14680064 | tf_op jit(solution)/shard_map/mixer_forward/pallas_call | solution.py:144
  167.0 9.3 %all-gather.8.cloned.1.call-done = bf16[1536,2048]{1,0:T(8,128)(2,1)} async-done(((bf16[1536,256]{1,0:T(8,128)(2,1)}), bf16[1536,2048]{1,0:T(8,128)(2,1)}) %all-gather.8.cloned.1.call-update) | async-done | bytes 6291472 | tf_op jit(solution)/shard_map/all_gather | solution.py:567
  191.0 22.4 %collective-permute-done.2 = bf16[256,2048]{1,0:T(8,128)(2,1)} collective-permute-done((bf16[256,2048]{1,0:T(8,128)(2,1)}, bf16[256,2048]{1,0:T(8,128)(2,1)}, u32[]{:S(2)}, u32[]{:S(2)}) %collective-permute-start.2) | collective-permute-done | bytes 1048608 | tf_op jit(solution)/shard_map/ppermute | solution.py:517
  220.5 9.0 %placed.3 = bf16[2048,1536]{1,0:T(8,128)(2,1)} custom-call(s32[8]{0:T(128)} %pad_add_fusion.2.ids_ref, bf16[1024,1536]{1,0:T(8,128)(2,1)} %collective-permute-done.12.far_ref, bf16[1024,1536]{1,0:T(8,128)(2,1)} %constant_dynamic-update-slice_fusion.5.near_ref), custom_call_target="tpu_custom_call" | custom-call | bytes 12582912 | tf_op jit(solution)/shard_map/placed/pallas_call | solution.py:416
  229.5 9.0 %placed.2 = bf16[2048,1536]{1,0:T(8,128)(2,1)} custom-call(s32[8]{0:T(128)} %pad_add_fusion.2.ids_ref, bf16[1024,1536]{1,0:T(8,128)(2,1)} %collective-permute-done.9.far_ref, bf16[1024,1536]{1,0:T(8,128)(2,1)} %constant_dynamic-update-slice_fusion.2.near_ref), custom_call_target="tpu_custom_call" | custom-call | bytes 12582912 | tf_op jit(solution)/shard_map/placed/pallas_call | solution.py:416
  265.6 22.0 %collective-permute-done.14.refs_2_ = bf16[256,2048]{1,0:T(8,128)(2,1)S(1)} collective-permute-done((bf16[256,2048]{1,0:T(8,128)(2,1)}, bf16[256,2048]{1,0:T(8,128)(2,1)S(1)}, u32[]{:S(2)}, u32[]{:S(2)}) %collective-permute-start.14) | collective-permute-done | bytes 1048608 | tf_op jit(solution)/shard_map/ppermute | solution.py:514
  296.6 34.3 %collective-permute-done.15.refs_3_ = bf16[256,2048]{1,0:T(8,128)(2,1)S(1)} collective-permute-done((bf16[256,2048]{1,0:T(8,128)(2,1)S(1)}, bf16[256,2048]{1,0:T(8,128)(2,1)S(1)}, u32[]{:S(2)}, u32[]{:S(2)}) %collective-permute-start.15) | collective-permute-done | bytes 1048608 | tf_op jit(solution)/shard_map/ppermute | solution.py:514
  358.3 18.7 %collective-permute-done.16 = bf16[256,2048]{1,0:T(8,128)(2,1)} collective-permute-done((bf16[256,2048]{1,0:T(8,128)(2,1)S(1)}, bf16[256,2048]{1,0:T(8,128)(2,1)}, u32[]{:S(2)}, u32[]{:S(2)}) %collective-permute-start.16) | collective-permute-done | bytes 1048608 | tf_op jit(solution)/shard_map/ppermute | solution.py:514
  380.4 9.7 %block_product.14 = (bf16[512,1536]{1,0:T(8,128)(2,1)}, f32[512,1536]{1,0:T(8,128)}) custom-call(s32[4]{0:T(128)} %copy-done.35, bf16[256,2048]{1,0:T(8,128)(2,1)} %refs_0_.2, bf16[256,2048]{1,0:T(8,128)(2,1)} %collective-permute-done.3.refs_1_, bf16[256,2048]{1,0:T(8,128)(2,1)} %collective-permute-done.4.refs_2_, ...), custom_call_target="tpu_custom_call" | custom-call | flops 3221225472 | bytes 11534336 | tf_op jit(solution)/shard_map/block_product/pallas_call | solution.py:327
  390.0 8.3 %block_product.15 = bf16[1024,1536]{1,0:T(8,128)(2,1)} custom-call(s32[4]{0:T(128)} %copy-done.36, bf16[256,2048]{1,0:T(8,128)(2,1)} %copy-done.28, bf16[256,2048]{1,0:T(8,128)(2,1)} %collective-permute-done.6.refs_1_, bf16[256,2048]{1,0:T(8,128)(2,1)} %copy-done.43, bf16[256,2048]{1,0:T(8,128)(2,1)} %copy-done.44, bf16[256,1536]{1,0:T(8,128)(2,1)} %copy-done.49, ...), custom_call_target="tpu_custom_call" | custom-call | flops 3221225472 | bytes 11534336 | tf_op jit(solution)/shard_map/block_product/pallas_call | solution.py:327
  398.4 8.6 %collective-permute-done.17 = bf16[256,2048]{1,0:T(8,128)(2,1)S(1)} collective-permute-done((bf16[256,2048]{1,0:T(8,128)(2,1)}, bf16[256,2048]{1,0:T(8,128)(2,1)S(1)}, u32[]{:S(2)}, u32[]{:S(2)}) %collective-permute-start.17) | collective-permute-done | bytes 1048608 | tf_op jit(solution)/shard_map/ppermute | solution.py:514
  416.4 9.7 %block_product.16 = (bf16[512,1536]{1,0:T(8,128)(2,1)}, f32[512,1536]{1,0:T(8,128)}) custom-call(s32[4]{0:T(128)} %copy-done.35, bf16[256,2048]{1,0:T(8,128)(2,1)} %copy-done.28, bf16[256,2048]{1,0:T(8,128)(2,1)} %collective-permute-done.6.refs_1_, bf16[256,2048]{1,0:T(8,128)(2,1)} %copy-done.43, bf16[256,2048]{1,0:T(8,128)(2,1)} %copy-done.44, ...), custom_call_target="tpu_custom_call" | custom-call | flops 3221225472 | bytes 11534336 | tf_op jit(solution)/shard_map/block_product/pallas_call | solution.py:327
  426.1 10.0 %collective-permute-done.19 = bf16[256,2048]{1,0:T(8,128)(2,1)S(1)} collective-permute-done((bf16[256,2048]{1,0:T(8,128)(2,1)}, bf16[256,2048]{1,0:T(8,128)(2,1)S(1)}, u32[]{:S(2)}, u32[]{:S(2)}) %collective-permute-start.19) | collective-permute-done | bytes 1048608 | tf_op jit(solution)/shard_map/ppermute | solution.py:517
  439.4 9.7 %block_product.17 = (bf16[512,1536]{1,0:T(8,128)(2,1)}, f32[512,1536]{1,0:T(8,128)}) custom-call(s32[4]{0:T(128)} %copy-done.35, bf16[256,2048]{1,0:T(8,128)(2,1)} %copy-done.28, bf16[256,2048]{1,0:T(8,128)(2,1)} %collective-permute-done.6.refs_1_, bf16[256,2048]{1,0:T(8,128)(2,1)} %copy-done.43, bf16[256,2048]{1,0:T(8,128)(2,1)} %copy-done.44, ...), custom_call_target="tpu_custom_call" | custom-call | flops 3221225472 | bytes 11534336 | tf_op jit(solution)/shard_map/block_product/pallas_call | solution.py:327
  449.1 18.0 %mixer_backward.2 = (bf16[512,1024]{1,0:T(8,128)(2,1)}, f32[8,128]{1,0:T(8,128)}, f32[512,2048]{1,0:T(8,128)}) custom-call(bf16[512,2048]{1,0:T(8,128)(2,1)} %pad_maximum_fusion.g_ref.refs_0_, bf16[2048,1536]{1,0:T(8,128)(2,1)} %all-gather.6.cloned.1.call-done.w_ref.o_ref, bf16[2048,1536]{1,0:T(8,128)(2,1)} %all-gather.6.cloned.1.call-done.w_ref.o_ref, ...), custom_call_target="tpu_custom_call" | custom-call | flops 4563402752 | bytes 14680064 | tf_op jit(solution)/shard_map/mixer_backward/pallas_call | solution.py:247
  484.4 21.5 %mixer_backward.3 = (bf16[512,1024]{1,0:T(8,128)(2,1)}, f32[8,128]{1,0:T(8,128)}, f32[256,2048]{1,0:T(8,128)}, bf16[256,2048]{1,0:T(8,128)(2,1)}, f32[1,2048]{1,0:T(1,128)}) custom-call(bf16[512,2048]{1,0:T(8,128)(2,1)} %pad_maximum_fusion.g_ref.refs_0_, bf16[2048,1536]{1,0:T(8,128)(2,1)} %all-gather.4.cloned.1.call-done.w_ref.o_ref, ...), custom_call_target="tpu_custom_call" | custom-call | flops 4563402752 | bytes 14680064 | tf_op jit(solution)/shard_map/mixer_backward/pallas_call | solution.py:247
  570.1 11.3 %collective-permute-done.39 = f32[4352]{0:T(1024)S(1)} collective-permute-done((f32[4352]{0:T(1024)S(1)}, f32[4352]{0:T(1024)S(1)}, u32[]{:S(2)}, u32[]{:S(2)}) %collective-permute-start.39) | collective-permute-done | bytes 17440 | tf_op jit(solution)/shard_map/ppermute | solution.py:715
  602.5 11.9 %collective-permute-done.34 = bf16[512,1024]{1,0:T(8,128)(2,1)} collective-permute-done((bf16[512,1024]{1,0:T(8,128)(2,1)}, bf16[512,1024]{1,0:T(8,128)(2,1)}, u32[]{:S(2)}, u32[]{:S(2)}) %collective-permute-start.34) | collective-permute-done | bytes 1048608 | tf_op jit(solution)/shard_map/ppermute | solution.py:460
  618.4 24.0 %collective-permute-done.33 = bf16[512,1024]{1,0:T(8,128)(2,1)S(1)} collective-permute-done((bf16[512,1024]{1,0:T(8,128)(2,1)}, bf16[512,1024]{1,0:T(8,128)(2,1)S(1)}, u32[]{:S(2)}, u32[]{:S(2)}) %collective-permute-start.33) | collective-permute-done | bytes 1048608 | tf_op jit(solution)/shard_map/ppermute | solution.py:460
  664.4 28.1 %collective-permute-done.46 = bf16[256,1536]{1,0:T(8,128)(2,1)S(1)} collective-permute-done((bf16[256,1536]{1,0:T(8,128)(2,1)S(1)}, bf16[256,1536]{1,0:T(8,128)(2,1)S(1)}, u32[]{:S(2)}, u32[]{:S(2)}) %collective-permute-start.46) | collective-permute-done | bytes 786464 | tf_op jit(solution)/shard_map/ppermute | solution.py:737
  (346 shorter events, 293.6 us)
Async XLA Ops:
  7.2 95.2 %all-gather.4.cloned.1.call-start = ((), (), s32[]{:S(2)}) async-start(), calls=%async_computation | async-start | bytes 7077888 | tf_op jit(solution)/shard_map/all_gather | solution.py:566
  14.6 132.0 %all-gather.6.cloned.1.call-start = ((), (), s32[]{:S(2)}) async-start(), calls=%async_computation.1 | async-start | bytes 7077888 | tf_op jit(solution)/shard_map/all_gather | solution.py:566
  14.7 43.1 %collective-permute-start = (bf16[256,2048]{1,0:T(8,128)(2,1)S(1)}, bf16[256,2048]{1,0:T(8,128)(2,1)S(1)}, u32[]{:S(2)}, u32[]{:S(2)}) collective-permute-start(bf16[256,2048]{1,0:T(8,128)(2,1)S(1)} %copy-done.1), channel_id=1, source_target_pairs={{0,1},{1,0},{2,3},{3,2},{4,5},{5,4},{6,7},{7,6},{8,9},{9,8},{10,11... | collective-permute-start | bytes 3145736 | tf_op jit(solution)/shard_map/ppermute | solution.py:517
  17.8 40.1 %collective-permute-start.1 = (bf16[256,1536]{1,0:T(8,128)(2,1)}, bf16[256,1536]{1,0:T(8,128)(2,1)}, u32[]{:S(2)}, u32[]{:S(2)}) collective-permute-start(bf16[256,1536]{1,0:T(8,128)(2,1)} %copy-done.25), channel_id=1, source_target_pairs={{0,2},{1,3},{2,0},{3,1},{4,6},{5,7},{6,4},{7,5},{8,10},{9,11},{10,... | collective-permute-start | bytes 2359304 | tf_op jit(solution)/shard_map/ppermute | solution.py:558
  58.0 118.4 %all-gather.8.cloned.1.call-start = ((), (), s32[]{:S(2)}) async-start(), calls=%async_computation.2 | async-start | bytes 7077888 | tf_op jit(solution)/shard_map/all_gather | solution.py:567
  73.6 45.5 %collective-permute-start.11 = (bf16[512,1536]{1,0:T(8,128)(2,1)}, bf16[512,1536]{1,0:T(8,128)(2,1)}, u32[]{:S(2)}, u32[]{:S(2)}) collective-permute-start(bf16[512,1536]{1,0:T(8,128)(2,1)} %pad_maximum_fusion.2), channel_id=1, source_target_pairs={{0,8},{4,20},{8,0},{12,28},{16,24},{20,4},{24,16},{28,12},{1,9},{5... | collective-permute-start | bytes 4718600 | tf_op jit(solution)/shard_map/ppermute | solution.py:396
  94.7 42.4 %collective-permute-start.8 = (bf16[512,1536]{1,0:T(8,128)(2,1)}, bf16[512,1536]{1,0:T(8,128)(2,1)}, u32[]{:S(2)}, u32[]{:S(2)}) collective-permute-start(bf16[512,1536]{1,0:T(8,128)(2,1)} %pad_maximum_fusion.1), channel_id=1, source_target_pairs={{0,8},{4,20},{8,0},{12,28},{16,24},{20,4},{24,16},{28,12},{1,9},{5... | collective-permute-start | bytes 4718600 | tf_op jit(solution)/shard_map/ppermute | solution.py:396
  124.9 95.6 %collective-permute-start.12 = (bf16[1024,1536]{1,0:T(8,128)(2,1)}, bf16[1024,1536]{1,0:T(8,128)(2,1)}, u32[]{:S(2)}, u32[]{:S(2)}) collective-permute-start(bf16[1024,1536]{1,0:T(8,128)(2,1)} %constant_dynamic-update-slice_fusion.5.near_ref), channel_id=1, source_target_pairs={{0,4},{4,0},{8,12},{12,8},{16,20},{20,16},{24,28},{28,24},{1,5},{5... | collective-permute-start | bytes 9437192 | tf_op jit(solution)/shard_map/ppermute | solution.py:396
  145.1 75.4 %collective-permute-start.9 = (bf16[1024,1536]{1,0:T(8,128)(2,1)}, bf16[1024,1536]{1,0:T(8,128)(2,1)}, u32[]{:S(2)}, u32[]{:S(2)}) collective-permute-start(bf16[1024,1536]{1,0:T(8,128)(2,1)} %constant_dynamic-update-slice_fusion.2.near_ref), channel_id=1, source_target_pairs={{0,4},{4,0},{8,12},{12,8},{16,20},{20,16},{24,28},{28,24},{1,5},{5... | collective-permute-start | bytes 9437192 | tf_op jit(solution)/shard_map/ppermute | solution.py:396
  164.8 50.7 %collective-permute-start.5 = (bf16[256,2048]{1,0:T(8,128)(2,1)}, bf16[256,2048]{1,0:T(8,128)(2,1)}, u32[]{:S(2)}, u32[]{:S(2)}) collective-permute-start(bf16[256,2048]{1,0:T(8,128)(2,1)} %collective-permute-done.4.refs_2_), channel_id=1, source_target_pairs={{0,1},{1,2},{2,3},{3,0},{4,5},{5,6},{6,7},{7,4},{8,9},{9,10},{10,1... | collective-permute-start | bytes 3145736 | tf_op jit(solution)/shard_map/ppermute | solution.py:514
  165.3 48.1 %collective-permute-start.2 = (bf16[256,2048]{1,0:T(8,128)(2,1)}, bf16[256,2048]{1,0:T(8,128)(2,1)}, u32[]{:S(2)}, u32[]{:S(2)}) collective-permute-start(bf16[256,2048]{1,0:T(8,128)(2,1)} %get-tuple-element.103), channel_id=1, source_target_pairs={{0,1},{1,0},{2,3},{3,2},{4,5},{5,4},{6,7},{7,6},{8,9},{9,8},{10,11... | collective-permute-start | bytes 3145736 | tf_op jit(solution)/shard_map/ppermute | solution.py:517
  265.5 75.5 %collective-permute-start.13 = (bf16[256,2048]{1,0:T(8,128)(2,1)S(1)}, bf16[256,2048]{1,0:T(8,128)(2,1)S(1)}, u32[]{:S(2)}, u32[]{:S(2)}) collective-permute-start(bf16[256,2048]{1,0:T(8,128)(2,1)S(1)} %convolution_add_fusion.2), channel_id=1, source_target_pairs={{0,1},{1,2},{2,3},{3,0},{4,5},{5,6},{6,7},{7,4},{8,9},{9,10},{10,1... | collective-permute-start | bytes 3145736 | tf_op jit(solution)/shard_map/ppermute | solution.py:514
  358.1 58.3 %collective-permute-start.23 = (bf16[1024,1536]{1,0:T(8,128)(2,1)}, bf16[1024,1536]{1,0:T(8,128)(2,1)}, u32[]{:S(2)}, u32[]{:S(2)}) collective-permute-start(bf16[1024,1536]{1,0:T(8,128)(2,1)} %block_product.13), channel_id=1, source_target_pairs={{0,4},{4,0},{8,12},{12,8},{16,20},{20,16},{24,28},{28,24},{1,5},{5... | collective-permute-start | bytes 9437192 | tf_op jit(solution)/shard_map/ppermute | solution.py:449
  398.3 41.1 %collective-permute-start.22 = (bf16[1024,1536]{1,0:T(8,128)(2,1)}, bf16[1024,1536]{1,0:T(8,128)(2,1)}, u32[]{:S(2)}, u32[]{:S(2)}) collective-permute-start(bf16[1024,1536]{1,0:T(8,128)(2,1)} %block_product.15), channel_id=1, source_target_pairs={{0,4},{4,0},{8,12},{12,8},{16,20},{20,16},{24,28},{28,24},{1,5},{5... | collective-permute-start | bytes 9437192 | tf_op jit(solution)/shard_map/ppermute | solution.py:449
  414.8 64.8 %collective-permute-start.21 = (bf16[512,1536]{1,0:T(8,128)(2,1)}, bf16[512,1536]{1,0:T(8,128)(2,1)}, u32[]{:S(2)}, u32[]{:S(2)}) collective-permute-start(bf16[512,1536]{1,0:T(8,128)(2,1)} %get-tuple-element.125), channel_id=1, source_target_pairs={{0,8},{4,20},{8,0},{12,28},{16,24},{20,4},{24,16},{28,12},{1,9},{5... | collective-permute-start | bytes 4718600 | tf_op jit(solution)/shard_map/ppermute | solution.py:460
  438.8 43.8 %collective-permute-start.20 = (bf16[256,2048]{1,0:T(8,128)(2,1)}, bf16[256,2048]{1,0:T(8,128)(2,1)}, u32[]{:S(2)}, u32[]{:S(2)}) collective-permute-start(bf16[256,2048]{1,0:T(8,128)(2,1)} %convolution_convert_fusion), channel_id=1, source_target_pairs={{0,1},{1,2},{2,3},{3,0},{4,5},{5,6},{6,7},{7,4},{8,9},{9,10},{10,1... | collective-permute-start | bytes 3145736 | tf_op jit(solution)/shard_map/ppermute | solution.py:514
  477.5 54.5 %collective-permute-start.30 = (bf16[512,1536]{1,0:T(8,128)(2,1)}, bf16[512,1536]{1,0:T(8,128)(2,1)}, u32[]{:S(2)}, u32[]{:S(2)}) collective-permute-start(bf16[512,1536]{1,0:T(8,128)(2,1)} %get-tuple-element.131), channel_id=1, source_target_pairs={{0,8},{4,20},{8,0},{12,28},{16,24},{20,4},{24,16},{28,12},{1,9},{5... | collective-permute-start | bytes 4718600 | tf_op jit(solution)/shard_map/ppermute | solution.py:460
  479.1 56.2 %collective-permute-start.29 = (bf16[512,1536]{1,0:T(8,128)(2,1)}, bf16[512,1536]{1,0:T(8,128)(2,1)}, u32[]{:S(2)}, u32[]{:S(2)}) collective-permute-start(bf16[512,1536]{1,0:T(8,128)(2,1)} %get-tuple-element.133), channel_id=1, source_target_pairs={{0,8},{4,20},{8,0},{12,28},{16,24},{20,4},{24,16},{28,12},{1,9},{5... | collective-permute-start | bytes 4718600 | tf_op jit(solution)/shard_map/ppermute | solution.py:460
  539.4 55.6 %collective-permute-start.35 = (bf16[256,2048]{1,0:T(8,128)(2,1)}, bf16[256,2048]{1,0:T(8,128)(2,1)}, u32[]{:S(2)}, u32[]{:S(2)}) collective-permute-start(bf16[256,2048]{1,0:T(8,128)(2,1)} %get-tuple-element.164), channel_id=1, source_target_pairs={{0,1},{1,0},{2,3},{3,2},{4,5},{5,4},{6,7},{7,6},{8,9},{9,8},{10,11... | collective-permute-start | bytes 3145736 | tf_op jit(solution)/shard_map/ppermute | solution.py:517
  588.5 55.6 %collective-permute-start.32 = (bf16[512,1024]{1,0:T(8,128)(2,1)}, bf16[512,1024]{1,0:T(8,128)(2,1)}, u32[]{:S(2)}, u32[]{:S(2)}) collective-permute-start(bf16[512,1024]{1,0:T(8,128)(2,1)} %get-tuple-element.155), channel_id=1, source_target_pairs={{0,8},{4,20},{8,0},{12,28},{16,24},{20,4},{24,16},{28,12},{1,9},{5... | collective-permute-start | bytes 3145736 | tf_op jit(solution)/shard_map/ppermute | solution.py:460
  590.0 57.0 %collective-permute-start.45 = (bf16[256,1536]{1,0:T(8,128)(2,1)}, bf16[256,1536]{1,0:T(8,128)(2,1)}, u32[]{:S(2)}, u32[]{:S(2)}) collective-permute-start(bf16[256,1536]{1,0:T(8,128)(2,1)} %slice.207), channel_id=1, source_target_pairs={{0,16},{4,12},{8,24},{12,4},{16,0},{20,28},{24,8},{28,20},{1,17},{... | collective-permute-start | bytes 2359304 | tf_op jit(solution)/shard_map/ppermute | solution.py:460
  594.3 56.4 %collective-permute-start.44 = (bf16[256,1536]{1,0:T(8,128)(2,1)}, bf16[256,1536]{1,0:T(8,128)(2,1)S(1)}, u32[]{:S(2)}, u32[]{:S(2)}) collective-permute-start(bf16[256,1536]{1,0:T(8,128)(2,1)} %slice.206), channel_id=1, source_target_pairs={{0,16},{4,12},{8,24},{12,4},{16,0},{20,28},{24,8},{28,20},{1,17},{... | collective-permute-start | bytes 2359304 | tf_op jit(solution)/shard_map/ppermute | solution.py:460
  595.1 47.2 %collective-permute-start.33 = (bf16[512,1024]{1,0:T(8,128)(2,1)}, bf16[512,1024]{1,0:T(8,128)(2,1)S(1)}, u32[]{:S(2)}, u32[]{:S(2)}) collective-permute-start(bf16[512,1024]{1,0:T(8,128)(2,1)} %get-tuple-element.157), channel_id=1, source_target_pairs={{0,8},{4,20},{8,0},{12,28},{16,24},{20,4},{24,16},{28,12},{1,9},{5... | collective-permute-start | bytes 3145736 | tf_op jit(solution)/shard_map/ppermute | solution.py:460
  614.3 48.6 %collective-permute-start.31 = (bf16[256,2048]{1,0:T(8,128)(2,1)S(1)}, bf16[256,2048]{1,0:T(8,128)(2,1)S(1)}, u32[]{:S(2)}, u32[]{:S(2)}) collective-permute-start(bf16[256,2048]{1,0:T(8,128)(2,1)S(1)} %copy-done.29), channel_id=1, source_target_pairs={{0,1},{1,2},{2,3},{3,0},{4,5},{5,6},{6,7},{7,4},{8,9},{9,10},{10,1... | collective-permute-start | bytes 3145736 | tf_op jit(solution)/shard_map/ppermute | solution.py:514
  (91 other events, 1255.0 us)
Sparse Core Ops, SparseCore 0:
  14.8 48.1 all-gather.3
  64.8 62.9 all-gather.5
  129.7 46.5 all-gather.7
